TPU v7x, 32 devices: a whole 2x2x4 slice. The times are simulated.
32 devices in a mesh: fsdp: 8 (over z, y), seq: 4 (over x, core).
Axes of the slice: x: 2, y: 2, z: 4, core: 2. Of those that a mesh axis runs over, the one named last changes fastest.
Arguments:
- tokens: bfloat16 [16, 1024, 1024], P('fsdp', 'seq'), may hold values from -6 to 6
- cotangent: bfloat16 [16, 1024, 1024], P('fsdp', 'seq'), may hold values from -6 to 6
- lengths: int32 [16], P('fsdp'), may hold values from 256 to 1024, as said below
- first_gain: bfloat16 [1024], P('fsdp'), may hold values from 0.25 to 1.75
- first_shift: bfloat16 [1024], P('fsdp'), may hold values from -3 to 3
- qkv_weight: bfloat16 [1024, 3072], P('fsdp'), may hold values from -0.1875 to 0.1875
- qv_bias: bfloat16 [2, 1024], P(None, 'fsdp'), may hold values from -3 to 3
- out_weight: bfloat16 [1024, 1024], P('fsdp'), may hold values from -0.375 to 0.375
- out_bias: bfloat16 [1024], P('fsdp'), may hold values from -2 to 2
- second_gain: bfloat16 [1024], P('fsdp'), may hold values from 0.25 to 1.75
- second_shift: bfloat16 [1024], P('fsdp'), may hold values from -3 to 3
- up_weight: bfloat16 [1024, 4096], P('fsdp'), may hold values from -0.1875 to 0.1875
- up_bias: bfloat16 [4096], P('fsdp'), may hold values from -3 to 3
- down_weight: bfloat16 [4096, 1024], P('fsdp'), may hold values from -0.09375 to 0.09375
- down_bias: bfloat16 [1024], P('fsdp'), may hold values from -2 to 2
Outputs:
- block_out: bfloat16 [16, 1024, 1024], P('fsdp', 'seq')
- tokens_grad: bfloat16 [16, 1024, 1024], P('fsdp', 'seq')
- first_gain_grad: float32 [1024], P(('fsdp', 'seq'))
- first_shift_grad: float32 [1024], P(('fsdp', 'seq'))
- qkv_weight_grad: float32 [1024, 3072], P(('fsdp', 'seq'))
- qv_bias_grad: float32 [2, 1024], P(None, ('fsdp', 'seq'))
- out_weight_grad: float32 [1024, 1024], P(('fsdp', 'seq'))
- out_bias_grad: float32 [1024], P(('fsdp', 'seq'))
- second_gain_grad: float32 [1024], P(('fsdp', 'seq'))
- second_shift_grad: float32 [1024], P(('fsdp', 'seq'))
- up_weight_grad: float32 [1024, 4096], P(('fsdp', 'seq'))
- up_bias_grad: float32 [4096], P(('fsdp', 'seq'))
- down_weight_grad: float32 [4096, 1024], P(('fsdp', 'seq'))
- down_bias_grad: float32 [1024], P(('fsdp', 'seq'))
Inputs may be any that keep to these rules, and one draw needn't show every extreme that they name: `lengths`: at least a quarter of 1024; in every draw some sequence has all 1024 slots valid.
All inputs are finite; a program needn't handle non-finite values.
Results may differ from a plain program's by a relative error of at most 0.011.
Values may be sent and summed in bfloat16 or wider, within the bound.
No kernel may reach another device: no remote copies, remote signals or barrier semaphores. Data moves between devices by JAX's collectives and lax.ppermute only.
A program may use at most 256 MiB of HBM per device.

v0:
```python
from functools import partial
import math

import jax
import jax.numpy as jnp
from jax import lax
from jax.experimental import pallas as pl
from jax.experimental.pallas import tpu as pltpu
from jax.sharding import PartitionSpec as P

H = 16


epsilon = 1e-05
f32 = jnp.float32
bf16 = jnp.bfloat16


def layer_norm(values, norm_gain, norm_shift):
    row_mean = jnp.mean(values, axis=-1, keepdims=True)
    centered = values - row_mean
    variance = jnp.mean(centered * centered, axis=-1, keepdims=True)
    return centered * lax.rsqrt(variance + epsilon) * norm_gain + norm_shift


def product(left_side, right_side):
    return jnp.dot(left_side, right_side, preferred_element_type=f32)


def contract_rows(left_side, right_side):
    return lax.dot_general(
        left_side, right_side, (((0,), (0,)), ((), ())), preferred_element_type=f32
    )


def against(left_side, right_side):
    return lax.dot_general(
        left_side, right_side, (((1,), (1,)), ((), ())), preferred_element_type=f32
    )


def head_scores(query_block, key_rows, start_row, slopes, length, score_scale):
    block_size = query_block.shape[1]
    seq_len = key_rows.shape[1]
    row_index = start_row + jnp.arange(block_size)
    columns = jnp.arange(seq_len)
    products = jnp.einsum("hqd,hkd->hqk", query_block, key_rows, preferred_element_type=f32)
    distance = (columns[None, :] - row_index[:, None]).astype(f32)
    allowed = (columns[None, :] <= row_index[:, None]) & (columns[None, :] < length)
    return jnp.where(
        allowed[None], products * score_scale + slopes[:, None, None] * distance, -jnp.inf
    )


def attend(queries, key_rows, value_rows, length, slopes, score_scale):
    head_count, seq_len, head_size = queries.shape
    block_size = math.gcd(512, seq_len)

    def one_block(start_row):
        query_block = lax.dynamic_slice_in_dim(queries, start_row, block_size, 1)
        scores = head_scores(query_block, key_rows, start_row, slopes, length, score_scale)
        largest = jnp.max(scores, axis=-1, keepdims=True)
        log_total = largest + jnp.log(jnp.sum(jnp.exp(scores - largest), axis=-1, keepdims=True))
        attention_probs = jnp.exp(scores - log_total).astype(bf16)
        mixed_rows = jnp.einsum(
            "hqk,hkd->hqd", attention_probs, value_rows, preferred_element_type=f32
        )
        return (mixed_rows.astype(bf16), log_total[..., 0])

    starts = jnp.arange(seq_len // block_size, dtype=jnp.int32) * block_size
    mixed_rows, log_totals = lax.map(one_block, starts)
    return (
        jnp.moveaxis(mixed_rows, 0, 1).reshape(head_count, seq_len, head_size),
        jnp.moveaxis(log_totals, 0, 1).reshape(head_count, seq_len),
    )


def attend_back(queries, key_rows, value_rows, grad_mixed, log_totals, length, slopes, score_scale):
    head_count, seq_len, head_size = queries.shape
    block_size = math.gcd(512, seq_len)

    def one_block(carried, start_row):
        key_sum, value_sum = carried
        query_block = lax.dynamic_slice_in_dim(queries, start_row, block_size, 1)
        grad_block = lax.dynamic_slice_in_dim(grad_mixed, start_row, block_size, 1)
        total_block = lax.dynamic_slice_in_dim(log_totals, start_row, block_size, 1)
        scores = head_scores(query_block, key_rows, start_row, slopes, length, score_scale)
        attention_probs = jnp.exp(scores - total_block[..., None])
        grad_probs = jnp.einsum(
            "hqd,hkd->hqk", grad_block, value_rows, preferred_element_type=f32
        )
        row_inner = jnp.sum(attention_probs * grad_probs, axis=-1, keepdims=True)
        grad_scores = (attention_probs * (grad_probs - row_inner)).astype(bf16)
        query_grad = (
            jnp.einsum("hqk,hkd->hqd", grad_scores, key_rows, preferred_element_type=f32)
            * score_scale
        ).astype(bf16)
        key_sum = (
            key_sum
            + jnp.einsum("hqk,hqd->hkd", grad_scores, query_block, preferred_element_type=f32)
            * score_scale
        )
        value_sum = value_sum + jnp.einsum(
            "hqk,hqd->hkd",
            attention_probs.astype(bf16),
            grad_block,
            preferred_element_type=f32,
        )
        return ((key_sum, value_sum), query_grad)

    starts = jnp.arange(seq_len // block_size, dtype=jnp.int32) * block_size
    empty = jnp.zeros(queries.shape, f32)
    (key_sum, value_sum), query_grads = lax.scan(one_block, (empty, empty), starts)
    query_grad = jnp.moveaxis(query_grads, 0, 1).reshape(head_count, seq_len, head_size)
    return (query_grad, key_sum.astype(bf16), value_sum.astype(bf16))


ACROSS = ((1,), (1,))
PLAIN = ((1,), (0,))
DOWN = ((0,), (0,))

def mm(left_side, right_side, dims):
    return lax.dot_general(left_side, right_side, (dims, ((), ())), preferred_element_type=f32)


def set_bias(length, head, su):
    rows = su.shape[1]
    u = lax.broadcasted_iota(jnp.int32, (rows, 128), 0)
    for h in range(2):
        power = jnp.full((rows, 128), head + (h + 1), jnp.int32).astype(f32)
        slope = jnp.exp2(power * (-8.0 / H))
        su[h] = jnp.where(u < length, u.astype(f32) * slope, -jnp.inf)


def half(value, h):
    lane = lax.broadcasted_iota(jnp.int32, value.shape, 1)
    return jnp.where((lane // 64) == h, value, jnp.zeros_like(value))


def scores(k_ref, q, h, su, nk, block):
    st = mm(k_ref[:nk], half(q, h) * jnp.asarray(0.125, bf16), ACROSS)
    st = st + jnp.concatenate([su[h, :nk]] * (block // 128), axis=1)
    keep = lax.broadcasted_iota(jnp.int32, (block, block), 0) <= lax.broadcasted_iota(
        jnp.int32, (block, block), 1
    )
    tail = jnp.where(keep, st[nk - block :], -jnp.inf)
    return tail if nk == block else jnp.concatenate([st[: nk - block], tail], axis=0)


def exchange(value, axis, bit):
    return lax.ppermute(value, axis, [(i, i ^ bit) for i in range(lax.axis_size(axis))])


def is_set(axis, bit):
    return (lax.axis_index(axis) // bit) % 2


def place(bit):
    return (0 if bit[0] == "fsdp" else 1, -bit[1])


def powers(size):
    return [1 << i for i in range(size.bit_length() - 1)]


def gather_bits(unit, order):
    held, buffer = [], unit
    for bit in order:
        received = exchange(buffer, *bit)
        second = is_set(*bit) == 1
        at = sum(1 for other in held if place(other) < place(bit))
        buffer = jnp.stack(
            [jnp.where(second, received, buffer), jnp.where(second, buffer, received)], axis=at
        )
        held.append(bit)
    return buffer


def scatter_bits(partial_sum, held, order):
    held, buffer = list(held), partial_sum
    for bit in order:
        at, mine = held.index(bit), is_set(*bit)
        sent = lax.dynamic_index_in_dim(buffer, 1 - mine, at, keepdims=False).astype(bf16)
        kept = lax.dynamic_index_in_dim(buffer, mine, at, keepdims=False).astype(f32)
        buffer = kept + exchange(sent, *bit).astype(f32)
        held.remove(bit)
    return buffer


def in_order(pieces, own):
    pieces = list(pieces)
    for bit in powers(len(pieces)):
        second = (own // bit) % 2 == 1
        pieces = [
            jnp.where(second, pieces[i ^ bit], pieces[i]) for i in range(len(pieces))
        ]
    return pieces


class Team:
    def __init__(self, micro_count):
        self.shards = lax.axis_size("seq")
        self.size = self.shards // micro_count
        self.micro_count = micro_count
        self.member = lax.axis_index("seq") % self.size
        self.which = lax.axis_index("seq") // self.size
        self.team_bits = [("seq", bit) for bit in powers(self.size)]
        self.pair_bits = [("seq", self.size * bit) for bit in powers(micro_count)]

    def to_sequences(self, pieces):
        arrived = []
        for offset in range(self.micro_count):
            sent = lax.dynamic_index_in_dim(pieces, self.which ^ offset, 0, keepdims=False)
            arrived.append(sent if offset == 0 else exchange(sent, "seq", offset * self.size))
        return jnp.stack(in_order(arrived, self.which))

    def share(self, own):
        arrived = [own if e == 0 else exchange(own, "seq", e) for e in range(self.size)]
        return jnp.stack(in_order(arrived, self.member), axis=1)

    def swap(self, pieces, axis, onto):
        arrived = []
        for e in range(self.size):
            sent = lax.dynamic_index_in_dim(pieces, self.member ^ e, axis, keepdims=False)
            arrived.append(sent if e == 0 else exchange(sent, "seq", e))
        return jnp.stack(in_order(arrived, self.member), axis=onto)

    def reduce(self, partial_sum):
        total = lax.dynamic_index_in_dim(partial_sum, self.member, 1, keepdims=False)
        for e in range(1, self.size):
            sent = lax.dynamic_index_in_dim(partial_sum, self.member ^ e, 1, keepdims=False)
            total = total + exchange(sent.astype(bf16), "seq", e).astype(f32)
        return total


def general_program(
    tokens,
    cotangent,
    lengths,
    first_gain,
    first_shift,
    qkv_weight,
    qv_bias,
    out_weight,
    out_bias,
    second_gain,
    second_shift,
    up_weight,
    up_bias,
    down_weight,
    down_bias,
):
    micro_count, block_rows, width = tokens.shape
    team = Team(micro_count)
    size, member, which = team.size, team.member, team.which
    shards = team.shards
    fsdp_shards = lax.axis_size("fsdp")
    seq_len = block_rows * shards
    head_size = width // H
    own_heads = H // size
    own_width = own_heads * head_size
    hidden = up_weight.shape[1]
    own_hidden = hidden // size
    fsdp_bits = [("fsdp", bit) for bit in powers(fsdp_shards)]
    line_bits = fsdp_bits[1:] + fsdp_bits[:1]
    pair_bits, team_bits = team.pair_bits, team.team_bits
    rows_first = lambda bits: sorted(bits, key=place)
    split = lambda bits: (2,) * len(bits)

    packed = jnp.concatenate(
        [
            first_gain,
            first_shift,
            second_gain,
            second_shift,
            out_bias,
            down_bias,
            qv_bias[0],
            qv_bias[1],
            up_bias,
        ]
    )
    packed = gather_bits(packed, line_bits).reshape(fsdp_shards, -1).astype(f32)
    part = width // fsdp_shards
    vectors = [packed[:, i * part : (i + 1) * part].reshape(width) for i in range(8)]
    gain_one, shift_one, gain_two, shift_two, bias_out, bias_down, bias_q, bias_v = vectors
    bias_up = packed[:, 8 * part :].reshape(hidden // (size * (hidden // (fsdp_shards * shards))), size, -1)
    bias_up = lax.dynamic_index_in_dim(bias_up, member, 1, keepdims=False).reshape(own_hidden)

    def part_rows(weight, bits, parts_of):
        rows = weight.shape[0] // parts_of
        index = jnp.int32(0)
        for bit in rows_first(bits):
            index = index * 2 + is_set(*bit)
        return lax.dynamic_slice_in_dim(weight, index * rows, rows, 0)

    qkv_own = lax.dynamic_slice_in_dim(qkv_weight, member * 3 * own_width, 3 * own_width, 1)
    qkv_own = jnp.swapaxes(qkv_own.reshape(-1, own_heads, 3, head_size), 1, 2).reshape(-1, 3 * own_width)
    whole_qkv = gather_bits(
        part_rows(qkv_own, pair_bits, micro_count), line_bits + pair_bits
    ).reshape(width, 3 * own_width)
    whole_out = gather_bits(
        part_rows(out_weight, pair_bits + team_bits, shards), line_bits + pair_bits + team_bits
    ).reshape(width, width)
    unit = hidden // (fsdp_shards * shards)
    up_own = lax.dynamic_index_in_dim(
        up_weight.reshape(width // fsdp_shards, hidden // (size * unit), size, unit),
        member,
        2,
        keepdims=False,
    ).reshape(width // fsdp_shards, own_hidden)
    whole_up = gather_bits(up_own, line_bits).reshape(width, own_hidden)
    down_own = lax.dynamic_index_in_dim(
        down_weight.reshape(micro_count, size, unit, width), member, 1, keepdims=False
    ).reshape(micro_count * unit, width)
    whole_down = gather_bits(
        part_rows(down_own, pair_bits, micro_count), line_bits + pair_bits
    ).reshape(own_hidden, width)

    length = lax.dynamic_index_in_dim(lengths, which, 0, keepdims=False)
    own_tokens = team.to_sequences(tokens)
    all_tokens = team.share(own_tokens).reshape(seq_len, width).astype(f32)
    own_rows = micro_count * block_rows
    own_tokens = own_tokens.reshape(own_rows, width).astype(f32)
    own_positions = (
        (jnp.arange(micro_count)[:, None] * size + member) * block_rows
        + jnp.arange(block_rows)[None, :]
    ).reshape(own_rows)
    valid_mask = (own_positions < length).astype(f32)[:, None]
    slopes = jnp.exp2(-((member * own_heads + jnp.arange(own_heads)).astype(f32) + 1.0) * 8.0 / H)
    score_scale = head_size ** (-0.5)

    by_member = (micro_count, size, block_rows)

    normed = layer_norm(all_tokens, gain_one, shift_one).astype(bf16)
    own_bias = lambda vector: lax.dynamic_slice_in_dim(vector, member * own_width, own_width, 0)
    bias_columns = jnp.concatenate([own_bias(bias_q), jnp.zeros((own_width,), f32), own_bias(bias_v)])
    projected = (product(normed, whole_qkv) + bias_columns).astype(bf16)
    split_heads = lambda value: jnp.moveaxis(value.reshape(seq_len, -1, head_size), 1, 0)
    join_heads = lambda value: jnp.moveaxis(value, 0, 1).reshape(seq_len, -1)
    queries, key_rows, value_rows = [
        split_heads(projected[:, i * own_width : (i + 1) * own_width]) for i in range(3)
    ]
    mixed, log_totals = attend(queries, key_rows, value_rows, length, slopes, score_scale)
    mixed = join_heads(mixed)
    mixed_rows = team.swap(mixed.reshape(by_member + (own_width,)), 1, 2).reshape(own_rows, width)
    middle = own_tokens + (product(mixed_rows, whole_out) + bias_out)
    normed_two_own = layer_norm(middle, gain_two, shift_two).astype(bf16)
    normed_two = team.share(normed_two_own.reshape(micro_count, block_rows, width)).reshape(
        seq_len, width
    )
    hidden_pre = product(normed_two, whole_up) + bias_up
    activation = jax.nn.gelu(hidden_pre, approximate=True).astype(bf16)
    fed = team.reduce(product(activation, whole_down).reshape(by_member + (width,)))
    block_own = (valid_mask * (middle + fed.reshape(own_rows, width) + bias_down)).astype(bf16)
    block_out = team.to_sequences(block_own.reshape(micro_count, block_rows, width))

    own_grad = team.to_sequences(cotangent)
    own_grad = jnp.where(
        (valid_mask > 0).reshape(micro_count, block_rows, 1), own_grad, jnp.zeros_like(own_grad)
    )
    grad_low = team.share(own_grad).reshape(seq_len, width)
    grad_out = own_grad.reshape(own_rows, width).astype(f32)
    down_bias_grad = jnp.sum(grad_out, axis=0)
    down_grad = contract_rows(activation, grad_low)
    grad_act = against(grad_low, whole_down)
    gelu_pull = jax.vjp(partial(jax.nn.gelu, approximate=True), hidden_pre)[1]
    grad_pre = gelu_pull(grad_act)[0].astype(bf16)
    up_grad = contract_rows(normed_two, grad_pre)
    up_bias_grad = jnp.sum(grad_pre.astype(f32), axis=0)
    grad_normed_two = team.reduce(
        against(grad_pre, whole_up).reshape(by_member + (width,))
    ).reshape(own_rows, width)
    norm_pull = jax.vjp(layer_norm, middle, gain_two, shift_two)[1]
    middle_part, second_gain_grad, second_shift_grad = norm_pull(grad_normed_two)
    grad_middle = grad_out + middle_part
    grad_branch = grad_middle.astype(bf16)
    out_bias_grad = jnp.sum(grad_branch.astype(f32), axis=0)
    out_grad = contract_rows(mixed_rows, grad_branch)
    grad_mixed_own = against(grad_branch, whole_out).astype(bf16)
    grad_mixed = team.swap(
        grad_mixed_own.reshape(micro_count, block_rows, size, own_width), 2, 1
    ).reshape(seq_len, own_width)
    backs = attend_back(
        queries,
        key_rows,
        value_rows,
        split_heads(grad_mixed),
        log_totals,
        length,
        slopes,
        score_scale,
    )
    grad_qkv = jnp.concatenate([join_heads(back) for back in backs], axis=1)
    qkv_grad = contract_rows(normed, grad_qkv)
    column_sums = jnp.sum(grad_qkv.astype(f32), axis=0).reshape(3, own_width)
    grad_normed = team.reduce(
        against(grad_qkv, whole_qkv).reshape(by_member + (width,))
    ).reshape(own_rows, width)
    first_pull = jax.vjp(layer_norm, own_tokens, gain_one, shift_one)[1]
    token_part, first_gain_grad, first_shift_grad = first_pull(grad_normed)
    row_grad = (grad_middle + token_part).astype(bf16)
    tokens_grad = team.to_sequences(row_grad.reshape(micro_count, block_rows, width))

    row_bits = rows_first(fsdp_bits + pair_bits)
    pair_first = pair_bits + fsdp_bits[:1] + fsdp_bits[:0:-1]
    pair_second = fsdp_bits[:1] + pair_bits + fsdp_bits[:0:-1]
    down_sum = scatter_bits(
        down_grad.reshape(split(row_bits) + (unit, width)), row_bits, pair_first
    )

    def by_columns(grad, order):
        total = scatter_bits(
            grad.reshape(split(row_bits) + (size, -1) + grad.shape[1:]), row_bits, order
        )
        return team.swap(total, 0, 1)

    up_sum = by_columns(up_grad, pair_second)
    up_sum = jnp.swapaxes(up_sum.reshape(-1, size, hidden // (size * unit), unit), 1, 2)
    up_sum = up_sum.reshape(-1, hidden)
    qkv_sum = by_columns(qkv_grad, pair_first).reshape(-1, size, 3, own_heads, head_size)
    qkv_sum = jnp.swapaxes(qkv_sum, 2, 3).reshape(-1, 3 * width)
    all_bits = rows_first(fsdp_bits + pair_bits + team_bits)
    out_sum = scatter_bits(
        out_grad.reshape(split(all_bits) + (-1, width)), all_bits, team_bits[::-1] + pair_first
    )

    devices = fsdp_shards * shards

    def spread(own, count):
        at_member = jnp.arange(size).reshape(1, size, 1) == member
        return jnp.where(at_member, own.reshape(count, 1, -1), 0.0)

    up_vector = spread(up_bias_grad, hidden // (size * unit)).reshape(devices, unit)
    by_team = lambda own: spread(own.reshape(1, own_width), 1).reshape(width)
    vectors = [
        first_gain_grad,
        first_shift_grad,
        second_gain_grad,
        second_shift_grad,
        out_bias_grad,
        down_bias_grad,
        by_team(column_sums[0]),
        by_team(column_sums[2]),
    ]
    buffer = jnp.concatenate([v.reshape(devices, -1) for v in vectors] + [up_vector], axis=1)
    buffer = buffer.reshape(split(all_bits) + (-1,))
    held = list(all_bits)
    for bit in team_bits + pair_first:
        at, mine = held.index(bit), is_set(*bit)
        sent = lax.dynamic_index_in_dim(buffer, 1 - mine, at, keepdims=False)
        kept = lax.dynamic_index_in_dim(buffer, mine, at, keepdims=False)
        buffer = kept + exchange(sent, *bit)
        held.remove(bit)
    each = width // devices
    sums = [buffer[i * each : (i + 1) * each] for i in range(8)]
    return (
        block_out,
        tokens_grad,
        sums[0],
        sums[1],
        qkv_sum,
        jnp.stack([sums[6], sums[7]]),
        out_sum,
        sums[4],
        sums[2],
        sums[3],
        up_sum,
        buffer[8 * each :],
        down_sum,
        sums[5],
    )


WORK = pl.CostEstimate(flops=10000000000, bytes_accessed=20000000, transcendentals=0)


def whole_block(array):
    return pl.BlockSpec(array.shape, lambda *_: (0,) * array.ndim, pipeline_mode=pl.Buffered(1))


def lanes(ref, block):
    return ref[:, pl.ds(pl.multiple_of(block * 128, 128), 128)]


def member_of(order):
    return order[1] & 1


def pair_of(order):
    return order[1] >> 1


def owner(order, i):
    return order[0] ^ ((i & 3) * 2 + (i >> 2))


def mixed_block(order, i):
    return owner(order, i) ^ (member_of(order) * 4 + pair_of(order) * 2)


def natural(order, i):
    return i


def picked(ref, order, first, block_of=owner):
    return jnp.concatenate([lanes(ref, block_of(order, first + i)) for i in range(4)], axis=1)


def flat(ref, start):
    value = ref[start : start + 4, :128]
    return value.reshape(512, value.shape[-1])


class Weight:
    def __init__(self, *parts, orders=None):
        self.parts = parts
        self.orders = orders or [owner] * len(parts)

    def slabs(self):
        found = []
        for pair in self.parts:
            for array, _, columns, which in pair:
                if not any(array is a and (columns, which) == b for a, b in found):
                    found.append((array, (columns, which)))
        return found

    def inputs(self):
        result = []
        for array, (columns, which) in self.slabs():
            spec = pl.BlockSpec(
                array.shape[:2] + (columns,),
                lambda *_, which=which: (0, 0, which),
                pipeline_mode=pl.Buffered(1),
            )
            result.append((array, spec))
        return result

    def tiles(self, columns=0, blocks=0):
        result = []
        for pair in self.parts:
            for array, first, wide, which in pair:
                if columns:
                    shape = (4, 128, columns)
                    place = lambda j, *_, f=first, w=which * (wide // columns): (f // 4, 0, w + j)
                else:
                    shape = (blocks, 128, wide)
                    place = lambda j, *_, f=first, w=which: (f // blocks + j, 0, w)
                result.append((array, pl.BlockSpec(shape, place)))
        return result

    def views(self, refs):
        slabs = self.slabs()

        def find(view):
            array, first, columns, which = view
            at = [array is a and (columns, which) == b for a, b in slabs].index(True)
            return refs[at], first

        return [(find(pair[0]), find(pair[1])) for pair in self.parts]


def grid_call(name, kernel, order, grid, inputs, outputs, scratch=(), limit=24):
    return pl.pallas_call(
        kernel,
        name=name,
        grid_spec=pltpu.PrefetchScalarGridSpec(
            num_scalar_prefetch=1,
            grid=grid,
            in_specs=[spec for _, spec in inputs],
            out_specs=[spec for _, spec in outputs],
            scratch_shapes=list(scratch),
        ),
        out_shape=[shape for shape, _ in outputs],
        compiler_params=pltpu.CompilerParams(vmem_limit_bytes=limit << 20),
        cost_estimate=WORK,
    )(order, *[a for a, _ in inputs])


def shape_of(shape, dtype):
    return jax.ShapeDtypeStruct(shape, dtype)


def normalized(values):
    row_mean = jnp.mean(values, axis=-1, keepdims=True)
    centered = values - row_mean
    rstd = lax.rsqrt(jnp.mean(centered * centered, axis=-1, keepdims=True) + epsilon)
    return centered * rstd, rstd


def first_norm(order, tokens, came, other_mine, other_came, vectors):
    _, block, width = tokens.shape

    def kernel(order, mine_ref, came_ref, other_mine_ref, other_came_ref, vec_ref, out_ref):
        def write(ref):
            xhat, _ = normalized(ref[...].astype(f32))
            out_ref[...] = (xhat * vec_ref[0:1] + vec_ref[1:2]).astype(bf16)

        at = pl.program_id(0)
        for i, ref in enumerate((mine_ref.at[0], came_ref, other_mine_ref, other_came_ref)):
            pl.when(at == i)(partial(write, ref))

    def place(i, o):
        return (((i % 2) ^ pair_of(o)) * 2 + ((i // 2) ^ member_of(o)), 0)

    return grid_call(
        "first_norm",
        kernel,
        order,
        (4,),
        [(tokens, pl.BlockSpec((1, block, width), lambda i, o: (pair_of(o), 0, 0)))]
        + [(a, whole_block(a)) for a in (came, other_mine, other_came, vectors)],
        [(shape_of((4 * block, width), bf16), pl.BlockSpec((block, width), place))],
    )[0]


def matrix(ref):
    value = ref[...]
    return value.reshape(value.shape[0] * value.shape[1], value.shape[2])


def project(order, normed, bias, part, weight, tile=256):
    rows, width = normed.shape
    columns = bias.shape[1]

    def kernel(order, lhs_ref, bias_ref, first_ref, second_ref, out_ref):
        total = mm(picked(lhs_ref, order, 0), matrix(first_ref), PLAIN)
        total = total + mm(picked(lhs_ref, order, 4), matrix(second_ref), PLAIN)
        out_ref[...] = (total + bias_ref[part : part + 1]).astype(bf16)

    return grid_call(
        "project",
        kernel,
        order,
        (columns // tile,),
        [(normed, whole_block(normed)), (bias, pl.BlockSpec((2, tile), lambda j, o: (0, j)))]
        + weight.tiles(columns=tile),
        [(shape_of((rows, columns), bf16), pl.BlockSpec((rows, tile), lambda j, o: (0, j)))],
    )[0]


def out_and_norm(order, mixed, tokens, vectors, weight, block=256):
    rows, width = mixed.shape

    def kernel(order, lhs_ref, tok_ref, vec_ref, *rest):
        middle_ref, norm_ref = rest[-2:]
        left = [picked(lhs_ref, order, i, mixed_block) for i in (0, 4)]
        for at, views in enumerate(weight.views(rest[:-2])):
            total = sum(mm(l, flat(*view), PLAIN) for l, view in zip(left, views))
            start = pl.multiple_of((member_of(order) ^ at) * (width // 2), 128)
            middle_ref[:, pl.ds(start, width // 2)] = total
        middle = tok_ref[...].astype(f32) + (middle_ref[...] + vec_ref[4:5])
        middle_ref[...] = middle
        xhat, _ = normalized(middle)
        norm_ref[...] = (xhat * vec_ref[2:3] + vec_ref[3:4]).astype(bf16)

    row = pl.BlockSpec((block, width), lambda i, o: (i, 0))
    return grid_call(
        "out_and_norm",
        kernel,
        order,
        (rows // block,),
        [(mixed, row), (tokens, row)]
        + [(vectors, whole_block(vectors))]
        + weight.inputs(),
        [(shape_of((rows, width), f32), row), (shape_of((rows, width), bf16), row)],
    )


ROOT = math.sqrt(2.0 / math.pi)


def gelu_and_slope(z):
    inner = jnp.tanh(ROOT * (z + 0.044715 * (z * z * z)))
    half_up = 0.5 * (1.0 + inner)
    slope = half_up + 0.5 * z * (1.0 - inner * inner) * (ROOT * (1.0 + 3 * 0.044715 * (z * z)))
    return z * half_up, slope


def feed_up(order, normed, bias, part, weight, tile=256):
    rows, width = normed.shape
    columns = bias.shape[1]

    def kernel(order, lhs_ref, bias_ref, first_ref, second_ref, act_ref, slope_ref):
        total = mm(picked(lhs_ref, order, 0), matrix(first_ref), PLAIN)
        total = total + mm(picked(lhs_ref, order, 4), matrix(second_ref), PLAIN)
        act, slope = gelu_and_slope(total + bias_ref[part : part + 1])
        act_ref[...] = act.astype(bf16)
        slope_ref[...] = slope.astype(bf16)

    out = pl.BlockSpec((rows, tile), lambda j, o: (0, j))
    return grid_call(
        "feed_up",
        kernel,
        order,
        (columns // tile,),
        [(normed, whole_block(normed)), (bias, pl.BlockSpec((2, tile), lambda j, o: (0, j)))]
        + weight.tiles(columns=tile),
        [(shape_of((rows, columns), bf16), out)] * 2,
    )


def own_and_sent(rows, width, tile):
    place = (lambda j, h, o: (0, j)) if tile < width else (lambda j, h, o: (0, 0))
    spec = pl.BlockSpec((rows, tile), place)
    return [(shape_of((rows, width), f32), spec), (shape_of((rows, width), bf16), spec)]


def half_rows(ref):
    rows = ref.shape[0] // 2
    return pl.ds(pl.multiple_of(pl.program_id(1) * rows, rows), rows)


def keep_or_send(own_ref, sent_ref, values):
    def save(ref):
        for where, value in values:
            ref[where] = value.astype(ref.dtype)

    pl.when(pl.program_id(1) == 0)(partial(save, own_ref))
    pl.when(pl.program_id(1) == 1)(partial(save, sent_ref))


def spread(order, totals):
    found = []
    for half, total in enumerate(totals):
        for k in range(2):
            block = owner(order, 4 * half + 2 * pl.program_id(0) + k)
            here = pl.ds(pl.multiple_of(block * 128, 128), 128)
            found.append(((slice(None), here), total[:, 128 * k : 128 * (k + 1)]))
    return found


def feed_down(order, acts, weight, tile=256):
    rows, columns = acts[0].shape
    width = 1024

    def kernel(order, first_act, second_act, *rest):
        weights, own_ref, sent_ref = rest[:4], rest[4], rest[5]
        here = half_rows(first_act)
        total = 0.0
        for part, act_ref in enumerate((first_act, second_act)):
            for half in range(2):
                left = picked(act_ref.at[here], order, 4 * half)
                total = total + mm(left, matrix(weights[2 * part + half]), PLAIN)
        keep_or_send(own_ref, sent_ref, [(Ellipsis, total)])

    return grid_call(
        "feed_down",
        kernel,
        order,
        (width // tile, 2),
        [(act, whole_block(act)) for act in acts] + weight.tiles(columns=tile),
        own_and_sent(rows // 2, width, tile),
    )


def feed_down_back(order, grad, slope, weight):
    rows, width = grad.shape
    columns = slope.shape[1]

    def kernel(order, lhs_ref, slope_ref, first_ref, second_ref, out_ref, sum_ref):
        @pl.when((pl.program_id(0) == 0) & (pl.program_id(1) == 0))
        def _():
            sum_ref[...] = jnp.zeros_like(sum_ref)

        here = half_rows(lhs_ref)
        left = lhs_ref[here]
        totals = [mm(left, matrix(ref), ACROSS) for ref in (first_ref, second_ref)]
        for (_, place), total in spread(order, totals):
            low = (total * slope_ref[here, place].astype(f32)).astype(bf16)
            out_ref[here, place] = low
            sum_ref[:, place] += rows_of_eight(low.astype(f32))

    return grid_call(
        "feed_down_back",
        kernel,
        order,
        (2, 2),
        [(grad, whole_block(grad)), (slope, whole_block(slope))] + weight.tiles(blocks=2),
        [
            (shape_of((rows, columns), bf16), pl.BlockSpec((rows, columns), lambda i, h, o: (0, 0))),
            (shape_of((8, columns), f32), pl.BlockSpec((8, columns), lambda i, h, o: (0, 0))),
        ],
    )


def feed_up_back(order, grads, weight):
    rows, columns = grads[0].shape
    width = 1024

    def kernel(order, first_grad, second_grad, *rest):
        weights, own_ref, sent_ref = rest[:4], rest[4], rest[5]
        here = half_rows(first_grad)
        totals = [
            mm(first_grad[here], matrix(weights[half]), ACROSS)
            + mm(second_grad[here], matrix(weights[2 + half]), ACROSS)
            for half in range(2)
        ]
        keep_or_send(own_ref, sent_ref, spread(order, totals))

    return grid_call(
        "feed_up_back",
        kernel,
        order,
        (2, 2),
        [(grad, whole_block(grad)) for grad in grads] + weight.tiles(blocks=2),
        own_and_sent(rows // 2, width, width),
    )


def rows_of_eight(value):
    return jnp.sum(value.reshape(value.shape[0] // 8, 8, value.shape[1]), axis=0)


def norm_back(xhat, rstd, grad_norm, gain):
    scaled = grad_norm * gain
    return rstd * (
        scaled
        - jnp.mean(scaled, axis=-1, keepdims=True)
        - xhat * jnp.mean(scaled * xhat, axis=-1, keepdims=True)
    )


def middle_back(order, own, came, middle, grad_out, vectors, weight, block=256):
    rows, width = middle.shape
    half_width = width // 2

    def kernel(order, own_ref, came_ref, middle_ref, dy_ref, vec_ref, *rest):
        grad_ref, branch_ref, keep_ref, sent_ref, sum_ref, tmp, low_ref = rest[-7:]

        @pl.when(pl.program_id(0) == 0)
        def _():
            sum_ref[...] = jnp.zeros_like(sum_ref)

        grad_norm = own_ref[...] + came_ref[...].astype(f32)
        xhat, rstd = normalized(middle_ref[...])
        grad_out = dy_ref[...].astype(f32)
        grad_middle = grad_out + norm_back(xhat, rstd, grad_norm, vec_ref[2:3])
        grad_ref[...] = grad_middle
        low = grad_middle.astype(bf16)
        low_ref[...] = low
        sum_ref[0] += rows_of_eight(grad_norm * xhat)
        sum_ref[1] += rows_of_eight(grad_norm)
        sum_ref[2] += rows_of_eight(low.astype(f32))
        sum_ref[3] += rows_of_eight(grad_out)
        views = weight.views(rest[:-7])
        member = member_of(order)
        for i in range(4):
            from_ = i ^ (member * 2 + pair_of(order))
            branch_ref[:, 256 * i : 256 * i + 256] = low_ref[:, pl.ds(pl.multiple_of(from_ * 256, 128), 256)]
        for half in range(2):
            total = 0.0
            for at, pair in enumerate(views):
                start = pl.multiple_of((member ^ at) * half_width, 128)
                total = total + mm(low_ref[:, pl.ds(start, half_width)], flat(*pair[half]), ACROSS)
            for k in range(4):
                here = pl.ds(pl.multiple_of(mixed_block(order, 4 * half + k) * 128, 128), 128)
                tmp[:, here] = total[:, 128 * k : 128 * (k + 1)].astype(bf16)
        keep_ref[...] = tmp[:, :half_width]
        sent_ref[...] = tmp[:, half_width:]

    row = pl.BlockSpec((block, width), lambda i, o: (i, 0))
    part = pl.BlockSpec((block, half_width), lambda i, o: (i, 0))
    return grid_call(
        "middle_back",
        kernel,
        order,
        (rows // block,),
        [(own, row), (came, row), (middle, row), (grad_out, row), (vectors, whole_block(vectors))]
        + weight.inputs(),
        [
            (shape_of((rows, width), f32), row),
            (shape_of((rows, width), bf16), row),
            (shape_of((rows, half_width), bf16), part),
            (shape_of((rows, half_width), bf16), part),
            (shape_of((4, 8, width), f32), pl.BlockSpec((4, 8, width), lambda i, o: (0, 0, 0))),
        ],
        scratch=[pltpu.VMEM((block, width), bf16)] * 2,
    )


def project_back(order, grads, weight):
    rows = grads[0][0].shape[0]
    block = rows // 4
    width = 1024
    given = [g for half in grads for g in half]

    def kernel(order, *rest):
        weights, own_ref, sent_ref = rest[6:10], rest[10], rest[11]

        def left(part):
            found = []
            for k in range(2):
                at = (k ^ pair_of(order)) * 2 + (pl.program_id(1) ^ member_of(order))
                here = pl.ds(pl.multiple_of(at * block, block), block)
                found.append(
                    jnp.concatenate([r[here] for r in rest[3 * part : 3 * part + 3]], axis=1)
                )
            return jnp.concatenate(found)

        lefts = [left(0), left(1)]
        totals = [
            mm(lefts[0], matrix(weights[half]), ACROSS)
            + mm(lefts[1], matrix(weights[2 + half]), ACROSS)
            for half in range(2)
        ]
        keep_or_send(own_ref, sent_ref, spread(order, totals))

    return grid_call(
        "project_back",
        kernel,
        order,
        (2, 2),
        [(g, whole_block(g)) for g in given] + weight.tiles(blocks=2),
        own_and_sent(rows // 2, width, width),
    )


def first_back(order, own, came, tokens, grad_middle, vectors, block=256):
    rows, width = own.shape

    def kernel(order, own_ref, came_ref, tok_ref, mid_ref, vec_ref, out_ref, sum_ref):
        @pl.when(pl.program_id(0) == 0)
        def _():
            sum_ref[...] = jnp.zeros_like(sum_ref)

        grad_norm = own_ref[...] + came_ref[...].astype(f32)
        xhat, rstd = normalized(tok_ref[...].astype(f32))
        total = mid_ref[...] + norm_back(xhat, rstd, grad_norm, vec_ref[0:1])
        out_ref[...] = total.astype(bf16)
        sum_ref[0] += rows_of_eight(grad_norm * xhat)
        sum_ref[1] += rows_of_eight(grad_norm)

    row = pl.BlockSpec((block, width), lambda i, o: (i, 0))
    return grid_call(
        "first_back",
        kernel,
        order,
        (rows // block,),
        [(own, row), (came, row), (tokens, row), (grad_middle, row), (vectors, whole_block(vectors))],
        [
            (shape_of((rows, width), bf16), row),
            (shape_of((2, 8, width), f32), pl.BlockSpec((2, 8, width), lambda i, o: (0, 0, 0))),
        ],
    )


def weight_grad(order, first, count, left, rights, block_of=owner, extra=None):
    wide = sum(columns for _, columns, _ in rights)
    extra = extra or ()
    more = extra[0].shape[2] if extra else 0
    together = 4

    def kernel(order, left_ref, *rest):
        right_refs, out_ref = rest[: len(rights)], rest[-1]
        at = first + together * pl.program_id(0)
        lefts = [lanes(left_ref, block_of(order, at + k)) for k in range(together)]
        picked_left = jnp.concatenate(lefts, axis=1)
        start = 0
        for ref in right_refs:
            total = mm(picked_left, ref[...], DOWN)
            width = total.shape[1]
            out_ref[:, :, start : start + width] = total.reshape(together, 128, width).astype(bf16)
            start += width
        if extra:
            kept, came = rest[len(rights) : -1]
            out_ref[:, :, start:] = (kept[...].astype(f32) + came[...].astype(f32)).astype(bf16)

    def right_spec(array, columns, which):
        return pl.BlockSpec(
            (array.shape[0], columns), lambda *_: (0, which), pipeline_mode=pl.Buffered(1)
        )

    def extra_spec(array, which):
        return pl.BlockSpec(
            (together, 128, more // 2), lambda i, o: (first // together + i, 0, which)
        )

    return grid_call(
        "weight_grad",
        kernel,
        order,
        (count // together,),
        [(left, whole_block(left))]
        + [(right[0], right_spec(*right)) for right in rights]
        + [(a, extra_spec(a, extra[2])) for a in extra[:2]],
        [
            (
                shape_of((count, 128, wide + more // 2), bf16),
                pl.BlockSpec((together, 128, wide + more // 2), lambda i, o: (i, 0, 0)),
            )
        ],
    )[0]


def head_of(order, part):
    return member_of(order) * 8 + (pair_of(order) ^ part) * 4 + 2 * pl.program_id(0)


def team_attend_kernel(part, order, q_ref, k_ref, v_ref, o_ref, total_ref, vt, su):
    at = pl.program_id(1)
    block = q_ref.shape[0]

    @pl.when(at == 0)
    def _():
        vt[...] = v_ref[...].T
        set_bias(order[2], head_of(order, part), su)

    def branch(b):
        nk = (b + 1) * block
        q = q_ref[...]
        outs, totals = [], []
        found = [scores(k_ref, q, h, su, nk, block) for h in range(2)]
        for h, st in enumerate(found):
            m = jnp.max(st, axis=0, keepdims=True)
            p = jnp.exp(st - m)
            l = jnp.sum(p, axis=0, keepdims=True)
            ot = mm(vt[64 * h : 64 * h + 64, :nk], p.astype(bf16), PLAIN)
            outs.append(ot / l)
            totals.append(m + jnp.log(l))
        o_ref[...] = jnp.concatenate(outs, axis=0).T.astype(bf16)
        total_ref[0] = jnp.concatenate(totals + [jnp.zeros((6, block), f32)], axis=0)

    for b in range(k_ref.shape[0] // block):
        pl.when(at == b)(partial(branch, b))


def kept_place(i, o):
    return ((i % 2) ^ member_of(o)) * 2 + ((i // 2) ^ pair_of(o))


def team_attend(order, qkv, part, block):
    rows = qkv.shape[0]
    whole = lambda kind: pl.BlockSpec((rows, 128), lambda p, i, o: (0, 2 * kind + p))
    return pl.pallas_call(
        partial(team_attend_kernel, part),
        name="team_attend",
        grid_spec=pltpu.PrefetchScalarGridSpec(
            num_scalar_prefetch=1,
            grid=(2, rows // block),
            in_specs=[pl.BlockSpec((block, 128), lambda p, i, o: (i, p)), whole(1), whole(2)],
            out_specs=[
                pl.BlockSpec((block, 128), lambda p, i, o: (kept_place(i, o), p)),
                pl.BlockSpec((1, 8, block), lambda p, i, o: (p, 0, i)),
            ],
            scratch_shapes=[pltpu.VMEM((128, rows), bf16), pltpu.VMEM((2, rows, 128), f32)],
        ),
        out_shape=[shape_of((rows, 256), bf16), shape_of((2, 8, rows), f32)],
        compiler_params=pltpu.CompilerParams(vmem_limit_bytes=16 << 20),
        cost_estimate=WORK,
    )(order, qkv, qkv, qkv)


def team_back_kernel(
    part, order, q_ref, k_ref, v_ref, g_ref, total_ref, dq_ref, dk_ref, dv_ref, sum_ref,
    kt, su, dk, dv
):
    at = pl.program_id(1)
    block = q_ref.shape[0]
    blocks = k_ref.shape[0] // block

    @pl.when(at == 0)
    def _():
        kt[...] = k_ref[...].T
        set_bias(order[2], head_of(order, part), su)
        dk[...] = jnp.zeros_like(dk)
        dv[...] = jnp.zeros_like(dv)
        sum_ref[...] = jnp.zeros_like(sum_ref)

    def branch(b):
        nk = (b + 1) * block
        q, g = q_ref[...], g_ref[...]
        outs, dks, dvs = [], [], []
        found = [scores(k_ref, q, h, su, nk, block) for h in range(2)]
        halves = [half(g, h) for h in range(2)]
        products = [mm(v_ref[:nk], gm, ACROSS) for gm in halves]
        for h in range(2):
            p = jnp.exp(found[h] - total_ref[0, h : h + 1])
            gm, dp = halves[h], products[h]
            inner = jnp.sum(p * dp, axis=0, keepdims=True)
            ds = (p * (dp - inner)).astype(bf16)
            outs.append(mm(kt[64 * h : 64 * h + 64, :nk], ds, PLAIN))
            dks.append(mm(ds, half(q, h), PLAIN))
            dvs.append(mm(p.astype(bf16), gm, PLAIN))
        low = (jnp.concatenate(outs, axis=0).T * 0.125).astype(bf16)
        dq_ref[...] = low
        sum_ref[0, 0] += rows_of_eight(low.astype(f32))
        dk[:nk] += dks[0] + dks[1]
        dv[:nk] += dvs[0] + dvs[1]

    for b in range(blocks):
        pl.when(at == b)(partial(branch, b))

    @pl.when(at == blocks - 1)
    def _():
        dk_ref[...] = (dk[...] * 0.125).astype(bf16)
        low = dv[...].astype(bf16)
        dv_ref[...] = low
        sum_ref[0, 1] = rows_of_eight(low.astype(f32))


def team_back(order, qkv, grad, totals, part, block):
    rows = qkv.shape[0]
    whole = lambda kind: pl.BlockSpec((rows, 128), lambda p, i, o: (0, 2 * kind + p))
    by_rows = pl.BlockSpec((block, 128), lambda p, i, o: (i, p))
    by_head = pl.BlockSpec((rows, 128), lambda p, i, o: (0, p))
    return pl.pallas_call(
        partial(team_back_kernel, part),
        name="team_back",
        grid_spec=pltpu.PrefetchScalarGridSpec(
            num_scalar_prefetch=1,
            grid=(2, rows // block),
            in_specs=[
                by_rows,
                whole(1),
                whole(2),
                pl.BlockSpec((block, 128), lambda p, i, o: (kept_place(i, o), 2 * part + p)),
                pl.BlockSpec((1, 8, block), lambda p, i, o: (p, 0, i)),
            ],
            out_specs=[
                by_rows,
                by_head,
                by_head,
                pl.BlockSpec((1, 2, 8, 128), lambda p, i, o: (p, 0, 0, 0)),
            ],
            scratch_shapes=[
                pltpu.VMEM((128, rows), bf16),
                pltpu.VMEM((2, rows, 128), f32),
                pltpu.VMEM((rows, 128), f32),
                pltpu.VMEM((rows, 128), f32),
            ],
        ),
        out_shape=[shape_of((rows, 256), bf16)] * 3 + [shape_of((2, 2, 8, 128), f32)],
        compiler_params=pltpu.CompilerParams(vmem_limit_bytes=24 << 20),
        cost_estimate=WORK,
    )(order, qkv, qkv, qkv, grad, totals)


def joined(first, second):
    count, rows, width = first.shape

    def kernel(first_ref, second_ref, out_ref):
        out_ref[:count] = first_ref[...]
        out_ref[count:] = second_ref[...]

    return pl.pallas_call(
        kernel,
        name="joined",
        out_shape=shape_of((2 * count, rows, width), first.dtype),
        compiler_params=pltpu.CompilerParams(vmem_limit_bytes=12 << 20),
        cost_estimate=WORK,
    )(first, second)


def qkv_unit(order, qkv_weight, packed):
    def kernel(order, qkv_ref, packed_ref, unit_ref):
        unit_ref[0, :128] = jnp.concatenate(
            [
                qkv_ref[:, n * 192 + kind * 64 : n * 192 + kind * 64 + 64]
                for kind in range(3)
                for n in range(4)
            ],
            axis=1,
        )
        unit_ref[0, 128:] = jnp.concatenate([packed_ref[...], jnp.zeros((16, 640), bf16)], axis=1)

    share = lambda i, o: (0, member_of(o) * 2 + pair_of(o))
    return grid_call(
        "qkv_unit",
        kernel,
        order,
        (1,),
        [(qkv_weight, pl.BlockSpec((128, 768), share)), (packed, whole_block(packed))],
        [(shape_of((1, 144, 768), bf16), pl.BlockSpec((1, 144, 768), lambda i, o: (0, 0, 0)))],
    )[0]


def other_units(order, out_weight, up_weight, down_weight):
    def kernel(order, out_ref, up_ref, down_ref, out_unit, own_unit, other_unit, down_unit):
        c, x = member_of(order), pair_of(order)
        out_unit[0] = out_ref[...]
        for i in range(8):
            own_unit[0, :, 128 * i : 128 * i + 128] = lanes(up_ref, i * 4 + x * 2 + c)
            other_unit[0, :, 128 * i : 128 * i + 128] = lanes(up_ref, i * 4 + (1 - x) * 2 + c)
        down_unit[0] = down_ref[...]

    shapes = [(1, 128, 512), (1, 128, 1024), (1, 128, 1024), (1, 128, 1024)]
    return grid_call(
        "other_units",
        kernel,
        order,
        (1,),
        [
            (out_weight, pl.BlockSpec((128, 512), lambda i, o: (0, member_of(o)))),
            (up_weight, whole_block(up_weight)),
            (down_weight, pl.BlockSpec((128, 1024), lambda i, o: (o[1], 0))),
        ],
        [(shape_of(s, bf16), pl.BlockSpec(s, lambda i, o: (0, 0, 0))) for s in shapes],
    )


def unpacked(order, mine, came):
    def kernel(order, mine_ref, came_ref, vec_ref, qkv_ref, up_ref, tmp):
        c, x = member_of(order), pair_of(order)
        for i in range(8):
            values = (mine_ref if i < 4 else came_ref)[i % 4].astype(f32)
            start = owner(order, i) * 128
            vec_ref[:, pl.ds(pl.multiple_of(start, 128), 128)] = values
            tmp[i] = values
            for part in range(2):
                row = tmp[i, pl.ds(8 + (x ^ part) * 2 + c, 1)]
                up_ref[part : part + 1, pl.ds(pl.multiple_of(start, 128), 128)] = row
        for part in range(2):
            here = pl.ds(pl.multiple_of(c * 512 + (x ^ part) * 256, 128), 256)
            qkv_ref[part : part + 1] = jnp.concatenate(
                [vec_ref[6:7, here], jnp.zeros((1, 256), f32), vec_ref[7:8, here]], axis=1
            )

    spec = pl.BlockSpec((4, 16, 128), lambda i, o: (0, 8, 0))
    shapes = [(16, 1024), (2, 768), (2, 1024)]
    return grid_call(
        "unpacked",
        kernel,
        order,
        (1,),
        [(mine, spec), (came, spec)],
        [(shape_of(s, f32), pl.BlockSpec(s, lambda i, o: (0, 0))) for s in shapes],
        scratch=[pltpu.VMEM((8, 16, 128), f32)],
    )


def vector_sums(order, middle, pre, heads, first):
    def kernel(order, middle_ref, pre_own, pre_other, own_ref, other_ref, first_ref, out_ref):
        c, x = member_of(order), pair_of(order)
        out_ref[...] = jnp.zeros_like(out_ref)
        for i in range(4):
            out_ref[i : i + 1] = jnp.sum(middle_ref[i], axis=0, keepdims=True)
        for i in range(2):
            out_ref[4 + i : 5 + i] = jnp.sum(first_ref[i], axis=0, keepdims=True)
        for part, ref in enumerate((own_ref, other_ref)):
            for pair in range(2):
                start = (c * 4 + (x ^ part) * 2 + pair) * 128
                here = pl.ds(pl.multiple_of(start, 128), 128)
                for kind in range(2):
                    total = jnp.sum(ref[pair, kind], axis=0, keepdims=True)
                    out_ref[6 + kind : 7 + kind, here] = total
        for part, ref in enumerate((pre_own, pre_other)):
            total = jnp.sum(ref[...], axis=0, keepdims=True)
            for i in range(8):
                start = (i % 2) * 512 + (x ^ part) * 256 + c * 128
                here = pl.ds(pl.multiple_of(start, 128), 128)
                row = 8 + i // 2
                out_ref[row : row + 1, here] = total[:, 128 * i : 128 * i + 128]

    arrays = (middle,) + tuple(pre) + tuple(heads) + (first,)
    return grid_call(
        "vector_sums",
        kernel,
        order,
        (1,),
        [(a, whole_block(a)) for a in arrays],
        [(shape_of((12, 1024), f32), pl.BlockSpec((12, 1024), lambda i, o: (0, 0)))],
    )[0]


def one_of(pair, index):
    return lax.dynamic_index_in_dim(pair, index, 0, keepdims=False)


def flipped(pair, index):
    return jnp.where(index == 0, pair, pair[::-1])


def after(value, *earlier):
    return lax.optimization_barrier((value,) + earlier)[0]


def team_program(
    tokens,
    cotangent,
    lengths,
    first_gain,
    first_shift,
    qkv_weight,
    qv_bias,
    out_weight,
    out_bias,
    second_gain,
    second_shift,
    up_weight,
    up_bias,
    down_weight,
    down_bias,
):
    _, block, width = tokens.shape
    own_rows = 2 * block
    f, s = lax.axis_index("fsdp"), lax.axis_index("seq")
    x, c = s // 2, s % 2
    over_x = lambda v: exchange(v, "seq", 2)
    over_y = lambda v: exchange(v, "fsdp", 1)
    over_z = lambda v, k: exchange(v, "fsdp", 2 * k)

    length = one_of(lengths, x)

    def over_core(value):
        return lax.cond(length > 0, lambda v: exchange(v, "seq", 1), lambda v: v, value)

    order = jnp.stack([f, s, length]).astype(jnp.int32)

    order = [jnp.stack([f, s, length]).astype(jnp.int32)]

    def wait_for(*values):
        order[0] = after(order[0], *values)

    def run(kernel, *operands, **options):
        result = kernel(order[0], *operands, **options)
        wait_for(result[0] if isinstance(result, (list, tuple)) else result)
        return result

    def join(first, second):
        result = joined(after(first, order[0]), second)
        wait_for(result)
        return result

    full = lambda a, b: ((a, 0, a.shape[2], 0), (b, 0, b.shape[2], 0))

    packed = [first_gain, first_shift, second_gain, second_shift, out_bias, down_bias, qv_bias, up_bias]
    packed = jnp.concatenate([v.reshape(-1, 128) for v in packed] + [jnp.zeros((4, 128), bf16)])
    unit_qkv = run(qkv_unit, qkv_weight, packed)
    tokens_came = over_x(one_of(tokens, 1 - x))
    unit_out, unit_up, unit_up_other, unit_down = run(
        other_units, out_weight, up_weight, down_weight
    )
    own_mine = one_of(tokens, x)
    other_mine, other_came = over_core(own_mine), over_core(tokens_came)
    grad_came = over_x(one_of(after(cotangent, tokens_came), 1 - x))
    z_qkv = join(unit_qkv, over_z(unit_qkv, 1))
    z_out = over_z(after(unit_out, z_qkv), 1)
    own_tokens = jnp.concatenate([own_mine, tokens_came])
    wait_for(other_mine, other_came)
    z_qkv = join(z_qkv, over_z(z_qkv, 2))
    y_qkv, xz_qkv = over_y(z_qkv), over_x(z_qkv)
    z_out = join(unit_out, z_out)
    z_out_came = over_z(z_out, 2)
    z_up = over_z(after(unit_up, z_out), 1)

    blocks_at = (jnp.arange(2) ^ x) * 2 + c
    valid = ((blocks_at[:, None] * block + jnp.arange(block)) < length).reshape(own_rows, 1)
    grad_own = jnp.concatenate([one_of(cotangent, x), grad_came])
    grad_own = jnp.where(valid, grad_own, jnp.zeros_like(grad_own))
    grad_other = over_core(grad_own)
    grad_all = jnp.concatenate([grad_own, grad_other])
    wait_for(grad_all)
    z_up = join(unit_up, z_up)
    z_up_came = over_z(z_up, 2)
    z_out = join(z_out, z_out_came)
    y_out = over_y(z_out)
    z_down = over_z(after(unit_down, z_up), 1)
    xy_qkv = over_x(y_qkv)
    qkv_own, qkv_other = full(z_qkv, y_qkv), full(xz_qkv, xy_qkv)
    vectors, bias_qkv, bias_up = run(unpacked, z_qkv, y_qkv)
    normed = run(first_norm, tokens, tokens_came, other_mine, other_came, vectors)
    projected = [None, None]
    mixed, totals = [None, None], [None, None]
    wait_for(xz_qkv)
    projected[0] = run(project, normed, bias_qkv, 0, Weight(qkv_own))
    mixed[0], totals[0] = run(team_attend, projected[0], 0, block)
    z_up = join(z_up, z_up_came)
    y_up = over_y(z_up)
    z_down = join(unit_down, z_down)
    z_down_came = over_z(z_down, 2)
    z_up_other = over_z(after(unit_up_other, z_down), 1)
    projected[1] = run(project, normed, bias_qkv, 1, Weight(qkv_other))
    mixed[1], totals[1] = run(team_attend, projected[1], 1, block)
    z_out_other, y_out_other = over_core(after(z_out, order[0])), over_core(after(y_out, order[0]))
    z_down = join(z_down, z_down_came)
    y_down, xz_down = over_y(z_down), over_x(z_down)
    z_up_other = join(unit_up_other, z_up_other)
    z_up_other_came = over_z(z_up_other, 2)
    out = Weight(full(z_out, y_out), full(z_out_other, y_out_other))
    sent = jnp.concatenate([m[own_rows:] for m in mixed], axis=1)
    mixed_rows = jnp.concatenate([m[:own_rows] for m in mixed] + [over_core(sent)], axis=1)
    middle, norm_own = run(out_and_norm, mixed_rows, own_tokens, vectors, out)
    norm_other = over_core(norm_own)
    wait_for(norm_other)
    norm_all = jnp.concatenate([norm_own, norm_other])

    act, slope, grad_pre, pre_sums = ([None, None] for _ in range(4))
    up_sent, up_kept, up_came = ([None, None] for _ in range(3))

    def up_grad(part, first):
        return run(weight_grad, first, 4, norm_all, [(grad_pre[part], 1024, 0)])

    def down_grad(part, first, count):
        return run(weight_grad, first, count, act[part], [(grad_all, 1024, 0)])

    act[0], slope[0] = run(feed_up, norm_all, bias_up, 0, Weight(full(z_up, y_up)))
    z_up_other = join(z_up_other, z_up_other_came)
    y_up_other = over_y(z_up_other)
    down_kept = down_grad(0, 0, 8)
    up = [full(z_up, y_up), full(z_up_other, y_up_other)]
    xy_down = over_x(y_down)
    down = [full(z_down, y_down), full(xz_down, xy_down)]
    grad_pre[0], pre_sums[0] = run(
        feed_down_back, grad_all, slope[0], Weight(down[0])
    )
    up_sent[0] = up_grad(0, 4)
    up_came[0] = over_y(up_sent[0])
    up_kept[0] = up_grad(0, 0)
    act[1], slope[1] = run(feed_up, norm_all, bias_up, 1, Weight(up[1]))
    down_sent = [None, None]
    for i in (1, 0):
        down_sent[i] = down_grad(1, 4 * i, 4)
    down_came = [over_x(sent) for sent in down_sent]
    grad_pre[1], pre_sums[1] = run(
        feed_down_back, grad_all, slope[1], Weight(down[1])
    )
    wait_for(up_came[0])
    up_sent[1] = up_grad(1, 4)
    up_came[1] = over_y(up_sent[1])
    back_own, back_sent = run(
        feed_up_back,
        grad_pre,
        Weight(*up),
    )
    back_came = over_core(back_sent)
    up_kept[1] = up_grad(1, 0)
    grad_middle, branch, mixed_kept, mixed_sent, middle_sums = run(
        middle_back, back_own, back_came, middle, grad_own, vectors, out
    )
    grad_mixed = jnp.concatenate([mixed_kept, over_core(mixed_sent)])
    out_grad = lambda which: run(
        weight_grad, 0, 8, mixed_rows, [(branch, 512, which)], block_of=mixed_block
    )
    out_sent = out_grad(1)
    out_came = over_core(out_sent)
    out_kept = out_grad(0)

    def added(kept, came):
        return kept.astype(f32) + came.astype(f32)

    def low_sum(kept, came):
        return added(kept, came).astype(bf16)

    def z_pieces(total):
        return [total[k].astype(bf16) for k in (1, 2, 3)]

    def sum_z(total, pieces):
        result = total[0]
        for k, piece in enumerate(pieces):
            result = result + over_z(piece, k + 1).astype(f32)
        return result

    def qkv_grad(grads, first, part):
        rights = [(grad, 256, 0) for grad in grads]
        return run(weight_grad, first, 4, normed, rights, extra=(out_kept, out_came, part))

    def z_far(total):
        return total[2:].astype(bf16)

    def z_near(total, far_came):
        total = added(total[:2], far_came)
        return total[0], total[1].astype(bf16)

    up_x = low_sum(up_kept[1], up_came[1])
    up_x_came = over_x(up_x)
    down_y = low_sum(down_kept[4:], down_came[1])
    down_y_came = over_y(down_y)
    wait_for(up_x, down_y)
    *heads_other, sums_other = run(team_back, projected[1], grad_mixed, totals[1], 1, block)
    other_y_came = over_y(qkv_grad(heads_other, 4, 1))
    down_total = added(low_sum(after(down_kept[:4], order[0]), down_came[0]), down_y_came)
    down_far = z_far(down_total)
    down_far_came = over_z(down_far, 2)
    wait_for(down_far)
    other_kept = qkv_grad(heads_other, 0, 1)
    *heads_own, sums_own = run(team_back, projected[0], grad_mixed, totals[0], 0, block)
    other_x = low_sum(other_kept, other_y_came)
    other_x_came = over_x(other_x)
    wait_for(other_x)
    own_y_came = over_y(qkv_grad(heads_own, 4, 0))
    up_total = added(low_sum(after(up_kept[0], order[0]), up_came[0]), up_x_came)
    up_far = z_far(up_total)
    up_far_came = over_z(up_far, 2)
    wait_for(up_far)
    first_own, first_sent = run(
        project_back, [heads_own, heads_other], Weight(qkv_own, qkv_other)
    )
    first_came = over_core(first_sent)
    fed_own, fed_sent = run(feed_down, act, Weight(*down))
    block_own = jnp.where(
        valid, middle + (fed_own + over_core(fed_sent).astype(f32)) + vectors[5:6], 0.0
    ).astype(bf16)
    down_sum, down_near = z_near(down_total, after(down_far_came, fed_own))
    down_near_came = over_z(down_near, 1)
    wait_for(down_near)
    up_sum, up_near = z_near(up_total, up_far_came)
    up_near_came = over_z(up_near, 1)
    wait_for(up_near, down_near_came)
    own_kept = qkv_grad(heads_own, 0, 0)
    qkv_total = added(own_kept, own_y_came) + other_x_came.astype(f32)
    qkv_pieces = z_pieces(qkv_total)
    wait_for(*qkv_pieces)
    row_grad, first_sums = run(first_back, first_own, first_came, own_tokens, grad_middle, vectors)

    def to_devices(rows):
        return flipped(jnp.stack([rows[:block], over_x(rows[block:])]), x)

    tokens_grad = to_devices(row_grad)
    block_out = to_devices(block_own)

    def over_pair(total):
        pieces = total.reshape(2, 64, -1)
        rows = flipped(jnp.stack([one_of(pieces, x), over_x(one_of(pieces, 1 - x))]), x)
        return jnp.swapaxes(rows, 0, 1)

    def over_team(total):
        pieces = total.reshape((2, 32) + total.shape[1:])
        rows = flipped(jnp.stack([one_of(pieces, c), over_core(one_of(pieces, 1 - c))]), c)
        return jnp.swapaxes(rows, 0, 1)

    down_sum = added(down_sum, down_near_came)
    up_sum = over_team(over_pair(added(up_sum, up_near_came)))
    up_sum = up_sum.reshape(32, 2, 2, 8, 128).transpose(0, 3, 2, 1, 4).reshape(32, 4096)
    qkv_sum = over_team(over_pair(sum_z(qkv_total, qkv_pieces)))
    out_sum = qkv_sum[..., 768:].reshape(32, width)
    qkv_sum = qkv_sum[..., :768].reshape(32, 2, 2, 3, 4, 64)
    qkv_sum = jnp.transpose(qkv_sum, (0, 1, 2, 4, 3, 5)).reshape(32, 3 * width)

    sums = run(vector_sums, middle_sums, pre_sums, (sums_own, sums_other), first_sums)
    for step in (over_core, over_x, over_y, partial(over_z, k=1), partial(over_z, k=2)):
        sums = sums + step(sums)
    place = f * 4 + s
    pieces = lax.dynamic_slice(sums[:8], (0, place * 32), (8, 32))
    up_piece = lax.dynamic_slice(sums[8:].reshape(4096), (place * 128,), (128,))
    return (
        block_out,
        tokens_grad,
        pieces[4],
        pieces[5],
        qkv_sum,
        pieces[6:8],
        out_sum,
        pieces[2],
        pieces[0],
        pieces[1],
        up_sum,
        up_piece,
        down_sum,
        pieces[3],
    )


def local(tokens, *others):
    width = tokens.shape[2]
    shards = (lax.axis_size("fsdp"), lax.axis_size("seq"))
    hidden = others[10].shape[1]
    if tokens.shape[0] == 2 and tokens.shape[1] % 256 == 0 and shards == (8, 4) and tokens.shape[1] * 4 <= 1024 and (width, hidden) == (1024, 4096):
        return team_program(tokens, *others)
    return general_program(tokens, *others)


def solution(mesh):
    return jax.shard_map(
        local,
        mesh=mesh,
        in_specs=(
            P("fsdp", "seq", None),
            P("fsdp", "seq", None),
            P("fsdp"),
            P("fsdp"),
            P("fsdp"),
            P("fsdp", None),
            P(None, "fsdp"),
            P("fsdp", None),
            P("fsdp"),
            P("fsdp"),
            P("fsdp"),
            P("fsdp", None),
            P("fsdp"),
            P("fsdp", None),
            P("fsdp"),
        ),
        out_specs=(
            P("fsdp", "seq", None),
            P("fsdp", "seq", None),
            P(("fsdp", "seq")),
            P(("fsdp", "seq")),
            P(("fsdp", "seq"), None),
            P(None, ("fsdp", "seq")),
            P(("fsdp", "seq"), None),
            P(("fsdp", "seq")),
            P(("fsdp", "seq")),
            P(("fsdp", "seq")),
            P(("fsdp", "seq"), None),
            P(("fsdp", "seq")),
            P(("fsdp", "seq"), None),
            P(("fsdp", "seq")),
        ),
        check_vma=False,
    )
```

profile of v0, /device:TPU:0, one launch (start us, length us, event | category | flops | bytes accessed | tf_op | source)
XLA Modules:
  0.0 398.6 jit_solution(12898267376979043365)
XLA Ops:
  28.6 7.9 %collective-permute-done.17.second_ref = bf16[2,144,768]{2,1,0:T(8,128)(2,1)S(1)} collective-permute-done((bf16[2,144,768]{2,1,0:T(8,128)(2,1)S(1)}, bf16[2,144,768]{2,1,0:T(8,128)(2,1)S(1)}, u32[]{:S(2)}, u32[]{:S(2)}) %collective-permute-start.17) | collective-permute-done | bytes 442400 | tf_op jit(solution)/shard_map/ppermute | solution.py:151
  39.4 4.0 %collective-permute-start.20 = (bf16[1,128,1024]{2,1,0:T(8,128)(2,1)}, bf16[1,128,1024]{2,1,0:T(8,128)(2,1)}, u32[]{:S(2)}, u32[]{:S(2)}) collective-permute-start(bf16[1,128,1024]{2,1,0:T(8,128)(2,1)} %get-tuple-element.263.first_ref), channel_id=1, source_target_pairs={{0,8},{4,12},{8,0},{12,4},{16,24},{20,28},{24,16},{28,20},{1,9},{5... | collective-permute-start | bytes 786440 | tf_op jit(solution)/shard_map/ppermute | solution.py:151
  61.1 3.6 first_norm.1.lhs_ref.left_ref
  67.7 8.2 %team_attend.2 = (bf16[1024,256]{1,0:T(8,128)(2,1)S(1)}, f32[2,8,1024]{2,1,0:T(8,128)S(1)}) custom-call(s32[3]{0:T(128)S(1)} %pad_add_fusion.order, bf16[1024,768]{1,0:T(8,128)(2,1)S(1)} %project.2.q_ref.k_ref.v_ref, bf16[1024,768]{1,0:T(8,128)(2,1)S(1)} %project.2.q_ref.k_ref.v_ref, bf16[1024,768]{1,0:T(8,128)(2,1)S(1)} %project.2.q_ref.k_ref.v_ref), custom_call_target="tpu_custom_call" | custom-call | flops 10000000000 | bytes 20000000 | tf_op jit(solution)/shard_map/team_attend/pallas_call | solution.py:1035
  80.1 3.4 collective-permute-start.28
  83.5 11.8 %collective-permute-done.26.second_ref.rest_9_ = bf16[4,144,768]{2,1,0:T(8,128)(2,1)S(1)} collective-permute-done((bf16[4,144,768]{2,1,0:T(8,128)(2,1)S(1)}, bf16[4,144,768]{2,1,0:T(8,128)(2,1)S(1)}, u32[]{:S(2)}, u32[]{:S(2)}) %collective-permute-start.26) | collective-permute-done | bytes 884768 | tf_op jit(solution)/shard_map/ppermute | solution.py:151
  95.3 4.0 %project.3.q_ref.k_ref.v_ref = bf16[1024,768]{1,0:T(8,128)(2,1)S(1)} custom-call(s32[3]{0:T(128)S(1)} %pad_add_fusion.order, bf16[1024,1024]{1,0:T(8,128)(2,1)S(1)} %first_norm.1.lhs_ref.left_ref, f32[2,768]{1,0:T(2,128)S(1)} %get-tuple-element.271.bias_ref, bf16[4,144,768]{2,1,0:T(8,128)(2,1)} %collective-permute-done.23.first_ref.rest_8_, ...), custom_call_target="tpu_custom_call" | custom-call | flops 10000000000 | bytes 20000000 | tf_op jit(solution)/shard_map/project/pallas_call | solution.py:564
  99.4 8.2 %team_attend.3 = (bf16[1024,256]{1,0:T(8,128)(2,1)S(1)}, f32[2,8,1024]{2,1,0:T(8,128)S(1)}) custom-call(s32[3]{0:T(128)S(1)} %pad_add_fusion.order, bf16[1024,768]{1,0:T(8,128)(2,1)S(1)} %project.3.q_ref.k_ref.v_ref, bf16[1024,768]{1,0:T(8,128)(2,1)S(1)} %project.3.q_ref.k_ref.v_ref, bf16[1024,768]{1,0:T(8,128)(2,1)S(1)} %project.3.q_ref.k_ref.v_ref), custom_call_target="tpu_custom_call" | custom-call | flops 10000000000 | bytes 20000000 | tf_op jit(solution)/shard_map/team_attend/pallas_call | solution.py:1035
  125.1 4.0 %out_and_norm.1 = (f32[512,1024]{1,0:T(8,128)S(1)}, bf16[512,1024]{1,0:T(8,128)(2,1)S(1)}) custom-call(s32[3]{0:T(128)S(1)} %pad_add_fusion.order, bf16[512,1024]{1,0:T(8,128)(2,1)S(1)} %pad_maximum_fusion.2.lhs_ref.left_ref, bf16[512,1024]{1,0:T(8,128)(2,1)S(1)} %pad_maximum_fusion.3.tok_ref, f32[16,1024]{1,0:T(8,128)S(1)} %get-tuple-element.267.vec_ref, ...), custom_call_target="tpu_custom_call" | custom-call | flops 10000000000 | bytes 20000000 | tf_op jit(solution)/shard_map/out_and_norm/pallas_call | solution.py:564
  131.5 3.2 conditional.21
  136.5 7.1 %feed_up.2 = (bf16[1024,1024]{1,0:T(8,128)(2,1)S(1)}, bf16[1024,1024]{1,0:T(8,128)(2,1)S(1)}) custom-call(s32[3]{0:T(128)S(1)} %pad_add_fusion.order, bf16[1024,1024]{1,0:T(8,128)(2,1)S(1)} %pad_maximum_fusion.1.lhs_ref.left_ref, f32[2,1024]{1,0:T(2,128)S(1)} %get-tuple-element.296.bias_ref, bf16[4,128,1024]{2,1,0:T(8,128)(2,1)S(1)} %joined.15.first_ref.rest_0_, ...), custom_call_target="tpu_custom_call" | custom-call | flops 10000000000 | bytes 20000000 | tf_op jit(solution)/shard_map/feed_up/pallas_call | solution.py:564
  146.3 3.2 weight_grad.13
  149.5 5.8 %feed_down_back.2 = (bf16[1024,1024]{1,0:T(8,128)(2,1)S(1)}, f32[8,1024]{1,0:T(8,128)S(1)}) custom-call(s32[3]{0:T(128)S(1)} %pad_add_fusion.order, bf16[1024,1024]{1,0:T(8,128)(2,1)S(1)} %copy-done.3, bf16[1024,1024]{1,0:T(8,128)(2,1)S(1)} %get-tuple-element.302.slope_ref, bf16[4,128,1024]{2,1,0:T(8,128)(2,1)} %joined.17.first_ref.rest_0_, ...), custom_call_target="tpu_custom_call" | custom-call | flops 10000000000 | bytes 20000000 | tf_op jit(solution)/shard_map/feed_down_back/pallas_call | solution.py:564
  161.4 10.3 %collective-permute-done.33.second_ref.rest_3_ = bf16[4,128,1024]{2,1,0:T(8,128)(2,1)S(1)} collective-permute-done((bf16[4,128,1024]{2,1,0:T(8,128)(2,1)S(1)}, bf16[4,128,1024]{2,1,0:T(8,128)(2,1)S(1)}, u32[]{:S(2)}, u32[]{:S(2)}) %collective-permute-start.33) | collective-permute-done | bytes 1048608 | tf_op jit(solution)/shard_map/ppermute | solution.py:151
  171.7 6.2 %feed_up.3 = (bf16[1024,1024]{1,0:T(8,128)(2,1)S(1)}, bf16[1024,1024]{1,0:T(8,128)(2,1)S(1)}) custom-call(s32[3]{0:T(128)S(1)} %pad_add_fusion.order, bf16[1024,1024]{1,0:T(8,128)(2,1)S(1)} %pad_maximum_fusion.1.lhs_ref.left_ref, f32[2,1024]{1,0:T(2,128)S(1)} %get-tuple-element.296.bias_ref, bf16[4,128,1024]{2,1,0:T(8,128)(2,1)S(1)} %joined.19.first_ref.rest_2_, ...), custom_call_target="tpu_custom_call" | custom-call | flops 10000000000 | bytes 20000000 | tf_op jit(solution)/shard_map/feed_up/pallas_call | solution.py:564
  186.7 5.3 %feed_down_back.3 = (bf16[1024,1024]{1,0:T(8,128)(2,1)S(1)}, f32[8,1024]{1,0:T(8,128)S(1)}) custom-call(s32[3]{0:T(128)S(1)} %pad_add_fusion.order, bf16[1024,1024]{1,0:T(8,128)(2,1)S(1)} %copy-done.3, bf16[1024,1024]{1,0:T(8,128)(2,1)S(1)} %get-tuple-element.311.slope_ref, bf16[4,128,1024]{2,1,0:T(8,128)(2,1)} %collective-permute-done.34.first_ref.rest_2_, ...), custom_call_target="tpu_custom_call" | custom-call | flops 10000000000 | bytes 20000000 | tf_op jit(solution)/shard_map/feed_down_back/pallas_call | solution.py:564
  196.6 8.4 %feed_up_back.1 = (f32[512,1024]{1,0:T(8,128)S(1)}, bf16[512,1024]{1,0:T(8,128)(2,1)}) custom-call(s32[3]{0:T(128)S(1)} %pad_add_fusion.order, bf16[1024,1024]{1,0:T(8,128)(2,1)S(1)} %get-tuple-element.303.rest_0_.first_grad, bf16[1024,1024]{1,0:T(8,128)(2,1)S(1)} %get-tuple-element.312.rest_0_.second_grad, bf16[4,128,1024]{2,1,0:T(8,128)(2,1)S(1)} %copy-done.28, ...), custom_call_target="tpu_custom_call" | custom-call | flops 10000000000 | bytes 20000000 | tf_op jit(solution)/shard_map/feed_up_back/pallas_call | solution.py:564
  206.4 3.9 conditional.22
  216.9 6.3 %middle_back.1 = (f32[512,1024]{1,0:T(8,128)S(1)}, bf16[512,1024]{1,0:T(8,128)(2,1)S(1)}, bf16[512,512]{1,0:T(8,128)(2,1)S(1)}, bf16[512,512]{1,0:T(8,128)(2,1)}, f32[4,8,1024]{2,1,0:T(8,128)S(1)}) custom-call(s32[3]{0:T(128)S(1)} %pad_add_fusion.order, f32[512,1024]{1,0:T(8,128)S(1)} %copy-done.44, bf16[512,1024]{1,0:T(8,128)(2,1)S(1)} %copy-done.105, ...), custom_call_target="tpu_custom_call" | custom-call | flops 10000000000 | bytes 20000000 | tf_op jit(solution)/shard_map/middle_back/pallas_call | solution.py:564
  240.6 12.5 %team_back.2 = (bf16[1024,256]{1,0:T(8,128)(2,1)S(1)}, bf16[1024,256]{1,0:T(8,128)(2,1)S(1)}, bf16[1024,256]{1,0:T(8,128)(2,1)S(1)}, f32[2,2,8,128]{3,2,1,0:T(8,128)S(1)}) custom-call(s32[3]{0:T(128)S(1)} %pad_add_fusion.order, bf16[1024,768]{1,0:T(8,128)(2,1)S(1)} %copy-done.59, bf16[1024,768]{1,0:T(8,128)(2,1)S(1)} %copy-done.59, ...), custom_call_target="tpu_custom_call" | custom-call | flops 10000000000 | bytes 20000000 | tf_op jit(solution)/shard_map/team_back/pallas_call | solution.py:1107
  257.7 5.5 %collective-permute-done.40 = bf16[4,128,1024]{2,1,0:T(8,128)(2,1)S(1)} collective-permute-done((bf16[4,128,1024]{2,1,0:T(8,128)(2,1)S(1)}, bf16[4,128,1024]{2,1,0:T(8,128)(2,1)S(1)}, u32[]{:S(2)}, u32[]{:S(2)}) %collective-permute-start.40) | collective-permute-done | bytes 1048608 | tf_op jit(solution)/shard_map/ppermute | solution.py:151
  270.6 12.7 %team_back.3 = (bf16[1024,256]{1,0:T(8,128)(2,1)S(1)}, bf16[1024,256]{1,0:T(8,128)(2,1)S(1)}, bf16[1024,256]{1,0:T(8,128)(2,1)S(1)}, f32[2,2,8,128]{3,2,1,0:T(8,128)S(1)}) custom-call(s32[3]{0:T(128)S(1)} %pad_add_fusion.order, bf16[1024,768]{1,0:T(8,128)(2,1)S(1)} %copy-done.57, bf16[1024,768]{1,0:T(8,128)(2,1)S(1)} %copy-done.57, ...), custom_call_target="tpu_custom_call" | custom-call | flops 10000000000 | bytes 20000000 | tf_op jit(solution)/shard_map/team_back/pallas_call | solution.py:1107
  286.3 3.6 weight_grad.24
  296.2 7.3 %project_back.1 = (f32[512,1024]{1,0:T(8,128)S(1)}, bf16[512,1024]{1,0:T(8,128)(2,1)}) custom-call(s32[3]{0:T(128)S(1)} %pad_add_fusion.order, bf16[1024,256]{1,0:T(8,128)(2,1)S(1)} %get-tuple-element.338.rest_0_, bf16[1024,256]{1,0:T(8,128)(2,1)S(1)} %get-tuple-element.341.rest_1_, bf16[1024,256]{1,0:T(8,128)(2,1)S(1)} %get-tuple-element.342.rest_2_, ...), custom_call_target="tpu_custom_call" | custom-call | flops 10000000000 | bytes 20000000 | tf_op jit(solution)/shard_map/project_back/pallas_call | solution.py:564
  304.8 9.4 %feed_down.1 = (f32[512,1024]{1,0:T(8,128)S(1)}, bf16[512,1024]{1,0:T(8,128)(2,1)}) custom-call(s32[3]{0:T(128)S(1)} %pad_add_fusion.order, bf16[1024,1024]{1,0:T(8,128)(2,1)S(1)} %copy-done.46, bf16[1024,1024]{1,0:T(8,128)(2,1)S(1)} %copy-done.48, bf16[4,128,1024]{2,1,0:T(8,128)(2,1)} %joined.17.first_ref.rest_0_, bf16[4,128,1024]{2,1,0:T(8,128)(2,1)S(1)} %copy-done.24, ...), custom_call_target="tpu_custom_call" | custom-call | flops 10000000000 | bytes 20000000 | tf_op jit(solution)/shard_map/feed_down/pallas_call | solution.py:564
  316.4 4.1 %collective-permute-start.46 = (bf16[128,1024]{1,0:T(8,128)(2,1)}, bf16[128,1024]{1,0:T(8,128)(2,1)}, u32[]{:S(2)}, u32[]{:S(2)}) collective-permute-start(bf16[128,1024]{1,0:T(8,128)(2,1)} %fusion.9), channel_id=1, source_target_pairs={{0,8},{4,12},{8,0},{12,4},{16,24},{20,28},{24,16},{28,20},{1,9},{5... | collective-permute-start | bytes 786440 | tf_op jit(solution)/shard_map/ppermute | solution.py:151
  320.5 3.8 conditional.25
  326.6 4.2 %conditional.26 = (bf16[512,1024]{1,0:T(8,128)(2,1)}) conditional(s32[]{:T(128)} %convert_element_type.138, bf16[512,1024]{1,0:T(8,128)(2,1)} %get-tuple-element.356, bf16[512,1024]{1,0:T(8,128)(2,1)} %get-tuple-element.356), branch_computations={%region_22.23_spmd, %region_23.24_spmd} | conditional | bytes 6291504 | solution.py:1306
  338.4 6.6 %collective-permute-done.43 = bf16[256,1024]{1,0:T(8,128)(2,1)S(1)} collective-permute-done((bf16[256,1024]{1,0:T(8,128)(2,1)S(1)}, bf16[256,1024]{1,0:T(8,128)(2,1)S(1)}, u32[]{:S(2)}, u32[]{:S(2)}) %collective-permute-start.43) | collective-permute-done | bytes 524320 | tf_op jit(solution)/shard_map/ppermute | solution.py:151
  347.9 3.9 fusion.11
  353.3 3.8 collective-permute-start.56
  368.4 3.9 collective-permute-done.51
  (448 shorter events, 238.3 us)
Async XLA Ops:
  3.2 20.7 %collective-permute-start.16 = (bf16[256,1024]{1,0:T(8,128)(2,1)}, bf16[256,1024]{1,0:T(8,128)(2,1)}, u32[]{:S(2)}, u32[]{:S(2)}) collective-permute-start(bf16[256,1024]{1,0:T(8,128)(2,1)} %get-tuple-element.374), channel_id=1, source_target_pairs={{0,2},{1,3},{2,0},{3,1},{4,6},{5,7},{6,4},{7,5},{8,10},{9,11},{10,... | collective-permute-start | bytes 1572872 | tf_op jit(solution)/shard_map/ppermute | solution.py:151
  15.2 21.3 %collective-permute-start.17 = (bf16[2,144,768]{2,1,0:T(8,128)(2,1)S(1)}, bf16[2,144,768]{2,1,0:T(8,128)(2,1)S(1)}, u32[]{:S(2)}, u32[]{:S(2)}) collective-permute-start(bf16[2,144,768]{2,1,0:T(8,128)(2,1)S(1)} %joined.10.first_ref), channel_id=1, source_target_pairs={{0,16},{4,20},{8,24},{12,28},{16,0},{20,4},{24,8},{28,12},{1,17},{... | collective-permute-start | bytes 1327112 | tf_op jit(solution)/shard_map/ppermute | solution.py:151
  24.7 18.7 %collective-permute-start.19 = (bf16[256,1024]{1,0:T(8,128)(2,1)}, bf16[256,1024]{1,0:T(8,128)(2,1)}, u32[]{:S(2)}, u32[]{:S(2)}) collective-permute-start(bf16[256,1024]{1,0:T(8,128)(2,1)} %dynamic-slice_bitcast_fusion.2), channel_id=1, source_target_pairs={{0,2},{1,3},{2,0},{3,1},{4,6},{5,7},{6,4},{7,5},{8,10},{9,11},{10,... | collective-permute-start | bytes 1572872 | tf_op jit(solution)/shard_map/ppermute | solution.py:151
  37.3 22.5 %collective-permute-start.22 = (bf16[4,144,768]{2,1,0:T(8,128)(2,1)S(1)}, bf16[4,144,768]{2,1,0:T(8,128)(2,1)S(1)}, u32[]{:S(2)}, u32[]{:S(2)}) collective-permute-start(bf16[4,144,768]{2,1,0:T(8,128)(2,1)S(1)} %joined.11.mine_ref.first_ref.rest_6_), channel_id=1, source_target_pairs={{0,4},{4,0},{8,12},{12,8},{16,20},{20,16},{24,28},{28,24},{1,5},{5... | collective-permute-start | bytes 2654216 | tf_op jit(solution)/shard_map/ppermute | solution.py:151
  38.9 25.8 %collective-permute-start.23 = (bf16[4,144,768]{2,1,0:T(8,128)(2,1)S(1)}, bf16[4,144,768]{2,1,0:T(8,128)(2,1)}, u32[]{:S(2)}, u32[]{:S(2)}) collective-permute-start(bf16[4,144,768]{2,1,0:T(8,128)(2,1)S(1)} %joined.11.mine_ref.first_ref.rest_6_), channel_id=1, source_target_pairs={{0,2},{1,3},{2,0},{3,1},{4,6},{5,7},{6,4},{7,5},{8,10},{9,11},{10,... | collective-permute-start | bytes 2654216 | tf_op jit(solution)/shard_map/ppermute | solution.py:151
  54.1 25.1 %collective-permute-start.24 = (bf16[2,128,1024]{2,1,0:T(8,128)(2,1)S(1)}, bf16[2,128,1024]{2,1,0:T(8,128)(2,1)S(1)}, u32[]{:S(2)}, u32[]{:S(2)}) collective-permute-start(bf16[2,128,1024]{2,1,0:T(8,128)(2,1)S(1)} %joined.13.first_ref), channel_id=1, source_target_pairs={{0,16},{4,20},{8,24},{12,28},{16,0},{20,4},{24,8},{28,12},{1,17},{... | collective-permute-start | bytes 1572872 | tf_op jit(solution)/shard_map/ppermute | solution.py:151
  56.7 57.1 %collective-permute-start.29 = (bf16[4,128,512]{2,1,0:T(8,128)(2,1)S(1)}, bf16[4,128,512]{2,1,0:T(8,128)(2,1)S(1)}, u32[]{:S(2)}, u32[]{:S(2)}) collective-permute-start(bf16[4,128,512]{2,1,0:T(8,128)(2,1)S(1)} %joined.14.rest_0_), channel_id=1, source_target_pairs={{0,4},{4,0},{8,12},{12,8},{16,20},{20,16},{24,28},{28,24},{1,5},{5... | collective-permute-start | bytes 1572872 | tf_op jit(solution)/shard_map/ppermute | solution.py:151
  57.7 21.6 %collective-permute-start.25 = (bf16[1,128,1024]{2,1,0:T(8,128)(2,1)S(1)}, bf16[1,128,1024]{2,1,0:T(8,128)(2,1)S(1)}, u32[]{:S(2)}, u32[]{:S(2)}) collective-permute-start(bf16[1,128,1024]{2,1,0:T(8,128)(2,1)S(1)} %copy-done.38), channel_id=1, source_target_pairs={{0,8},{4,12},{8,0},{12,4},{16,24},{20,28},{24,16},{28,20},{1,9},{5... | collective-permute-start | bytes 786440 | tf_op jit(solution)/shard_map/ppermute | solution.py:151
  75.9 19.4 %collective-permute-start.26 = (bf16[4,144,768]{2,1,0:T(8,128)(2,1)S(1)}, bf16[4,144,768]{2,1,0:T(8,128)(2,1)S(1)}, u32[]{:S(2)}, u32[]{:S(2)}) collective-permute-start(bf16[4,144,768]{2,1,0:T(8,128)(2,1)S(1)} %collective-permute-done.22.came_ref.second_ref.rest_7_), channel_id=1, source_target_pairs={{0,2},{1,3},{2,0},{3,1},{4,6},{5,7},{6,4},{7,5},{8,10},{9,11},{10,... | collective-permute-start | bytes 2654216 | tf_op jit(solution)/shard_map/ppermute | solution.py:151
  79.3 28.3 %collective-permute-start.27 = (bf16[2,128,1024]{2,1,0:T(8,128)(2,1)S(1)}, bf16[2,128,1024]{2,1,0:T(8,128)(2,1)S(1)}, u32[]{:S(2)}, u32[]{:S(2)}) collective-permute-start(bf16[2,128,1024]{2,1,0:T(8,128)(2,1)S(1)} %joined.16.first_ref), channel_id=1, source_target_pairs={{0,16},{4,20},{8,24},{12,28},{16,0},{20,4},{24,8},{28,12},{1,17},{... | collective-permute-start | bytes 1572872 | tf_op jit(solution)/shard_map/ppermute | solution.py:151
  79.4 57.1 %collective-permute-start.30 = (bf16[4,128,1024]{2,1,0:T(8,128)(2,1)S(1)}, bf16[4,128,1024]{2,1,0:T(8,128)(2,1)}, u32[]{:S(2)}, u32[]{:S(2)}) collective-permute-start(bf16[4,128,1024]{2,1,0:T(8,128)(2,1)S(1)} %joined.15.first_ref.rest_0_), channel_id=1, source_target_pairs={{0,4},{4,0},{8,12},{12,8},{16,20},{20,16},{24,28},{28,24},{1,5},{5... | collective-permute-start | bytes 3145736 | tf_op jit(solution)/shard_map/ppermute | solution.py:151
  80.1 28.6 %collective-permute-start.28 = (bf16[1,128,1024]{2,1,0:T(8,128)(2,1)S(1)}, bf16[1,128,1024]{2,1,0:T(8,128)(2,1)S(1)}, u32[]{:S(2)}, u32[]{:S(2)}) collective-permute-start(bf16[1,128,1024]{2,1,0:T(8,128)(2,1)S(1)} %get-tuple-element.288.first_ref), channel_id=1, source_target_pairs={{0,8},{4,12},{8,0},{12,4},{16,24},{20,28},{24,16},{28,20},{1,9},{5... | collective-permute-start | bytes 786440 | tf_op jit(solution)/shard_map/ppermute | solution.py:151
  109.5 34.1 %collective-permute-start.31 = (bf16[2,128,1024]{2,1,0:T(8,128)(2,1)}, bf16[2,128,1024]{2,1,0:T(8,128)(2,1)}, u32[]{:S(2)}, u32[]{:S(2)}) collective-permute-start(bf16[2,128,1024]{2,1,0:T(8,128)(2,1)} %joined.18.first_ref), channel_id=1, source_target_pairs={{0,16},{4,20},{8,24},{12,28},{16,0},{20,4},{24,8},{28,12},{1,17},{... | collective-permute-start | bytes 1572872 | tf_op jit(solution)/shard_map/ppermute | solution.py:151
  110.1 39.3 %collective-permute-start.32 = (bf16[4,128,1024]{2,1,0:T(8,128)(2,1)}, bf16[4,128,1024]{2,1,0:T(8,128)(2,1)S(1)}, u32[]{:S(2)}, u32[]{:S(2)}) collective-permute-start(bf16[4,128,1024]{2,1,0:T(8,128)(2,1)} %joined.17.first_ref.rest_0_), channel_id=1, source_target_pairs={{0,4},{4,0},{8,12},{12,8},{16,20},{20,16},{24,28},{28,24},{1,5},{5... | collective-permute-start | bytes 3145736 | tf_op jit(solution)/shard_map/ppermute | solution.py:151
  111.7 74.1 %collective-permute-start.34 = (bf16[4,128,1024]{2,1,0:T(8,128)(2,1)}, bf16[4,128,1024]{2,1,0:T(8,128)(2,1)}, u32[]{:S(2)}, u32[]{:S(2)}) collective-permute-start(bf16[4,128,1024]{2,1,0:T(8,128)(2,1)} %joined.17.first_ref.rest_0_), channel_id=1, source_target_pairs={{0,2},{1,3},{2,0},{3,1},{4,6},{5,7},{6,4},{7,5},{8,10},{9,11},{10,... | collective-permute-start | bytes 3145736 | tf_op jit(solution)/shard_map/ppermute | solution.py:151
  145.7 26.1 %collective-permute-start.33 = (bf16[4,128,1024]{2,1,0:T(8,128)(2,1)S(1)}, bf16[4,128,1024]{2,1,0:T(8,128)(2,1)S(1)}, u32[]{:S(2)}, u32[]{:S(2)}) collective-permute-start(bf16[4,128,1024]{2,1,0:T(8,128)(2,1)S(1)} %joined.19.first_ref.rest_2_), channel_id=1, source_target_pairs={{0,4},{4,0},{8,12},{12,8},{16,20},{20,16},{24,28},{28,24},{1,5},{5... | collective-permute-start | bytes 3145736 | tf_op jit(solution)/shard_map/ppermute | solution.py:151
  157.1 36.3 %collective-permute-start.36 = (bf16[4,128,1024]{2,1,0:T(8,128)(2,1)S(1)}, bf16[4,128,1024]{2,1,0:T(8,128)(2,1)S(1)}, u32[]{:S(2)}, u32[]{:S(2)}) collective-permute-start(bf16[4,128,1024]{2,1,0:T(8,128)(2,1)S(1)} %weight_grad.14), channel_id=1, source_target_pairs={{0,4},{4,0},{8,12},{12,8},{16,20},{20,16},{24,28},{28,24},{1,5},{5... | collective-permute-start | bytes 3145736 | tf_op jit(solution)/shard_map/ppermute | solution.py:151
  160.6 26.1 %collective-permute-start.35 = (bf16[4,128,1024]{2,1,0:T(8,128)(2,1)S(1)}, bf16[4,128,1024]{2,1,0:T(8,128)(2,1)S(1)}, u32[]{:S(2)}, u32[]{:S(2)}) collective-permute-start(bf16[4,128,1024]{2,1,0:T(8,128)(2,1)S(1)} %copy-done.23), channel_id=1, source_target_pairs={{0,2},{1,3},{2,0},{3,1},{4,6},{5,7},{6,4},{7,5},{8,10},{9,11},{10,... | collective-permute-start | bytes 3145736 | tf_op jit(solution)/shard_map/ppermute | solution.py:151
  180.9 54.2 %collective-permute-start.38 = (bf16[4,128,1024]{2,1,0:T(8,128)(2,1)}, bf16[4,128,1024]{2,1,0:T(8,128)(2,1)}, u32[]{:S(2)}, u32[]{:S(2)}) collective-permute-start(bf16[4,128,1024]{2,1,0:T(8,128)(2,1)} %weight_grad.16), channel_id=1, source_target_pairs={{0,2},{1,3},{2,0},{3,1},{4,6},{5,7},{6,4},{7,5},{8,10},{9,11},{10,... | collective-permute-start | bytes 3145736 | tf_op jit(solution)/shard_map/ppermute | solution.py:151
  184.5 73.2 %collective-permute-start.39 = (bf16[4,128,1024]{2,1,0:T(8,128)(2,1)}, bf16[4,128,1024]{2,1,0:T(8,128)(2,1)}, u32[]{:S(2)}, u32[]{:S(2)}) collective-permute-start(bf16[4,128,1024]{2,1,0:T(8,128)(2,1)} %weight_grad.17), channel_id=1, source_target_pairs={{0,2},{1,3},{2,0},{3,1},{4,6},{5,7},{6,4},{7,5},{8,10},{9,11},{10,... | collective-permute-start | bytes 3145736 | tf_op jit(solution)/shard_map/ppermute | solution.py:151
  196.3 42.6 %collective-permute-start.37 = (bf16[4,128,1024]{2,1,0:T(8,128)(2,1)}, bf16[4,128,1024]{2,1,0:T(8,128)(2,1)}, u32[]{:S(2)}, u32[]{:S(2)}) collective-permute-start(bf16[4,128,1024]{2,1,0:T(8,128)(2,1)} %weight_grad.18), channel_id=1, source_target_pairs={{0,4},{4,0},{8,12},{12,8},{16,20},{20,16},{24,28},{28,24},{1,5},{5... | collective-permute-start | bytes 3145736 | tf_op jit(solution)/shard_map/ppermute | solution.py:151
  237.2 26.1 %collective-permute-start.40 = (bf16[4,128,1024]{2,1,0:T(8,128)(2,1)S(1)}, bf16[4,128,1024]{2,1,0:T(8,128)(2,1)S(1)}, u32[]{:S(2)}, u32[]{:S(2)}) collective-permute-start(bf16[4,128,1024]{2,1,0:T(8,128)(2,1)S(1)} %add_convert_fusion.3), channel_id=1, source_target_pairs={{0,4},{4,0},{8,12},{12,8},{16,20},{20,16},{24,28},{28,24},{1,5},{5... | collective-permute-start | bytes 3145736 | tf_op jit(solution)/shard_map/ppermute | solution.py:151
  256.4 28.5 %collective-permute-start.41 = (bf16[4,128,1024]{2,1,0:T(8,128)(2,1)S(1)}, bf16[4,128,1024]{2,1,0:T(8,128)(2,1)S(1)}, u32[]{:S(2)}, u32[]{:S(2)}) collective-permute-start(bf16[4,128,1024]{2,1,0:T(8,128)(2,1)S(1)} %weight_grad.22), channel_id=1, source_target_pairs={{0,4},{4,0},{8,12},{12,8},{16,20},{20,16},{24,28},{28,24},{1,5},{5... | collective-permute-start | bytes 3145736 | tf_op jit(solution)/shard_map/ppermute | solution.py:151
  256.8 33.1 %collective-permute-start.42 = (bf16[4,128,1024]{2,1,0:T(8,128)(2,1)S(1)}, bf16[4,128,1024]{2,1,0:T(8,128)(2,1)S(1)}, u32[]{:S(2)}, u32[]{:S(2)}) collective-permute-start(bf16[4,128,1024]{2,1,0:T(8,128)(2,1)S(1)} %add_convert_fusion.4), channel_id=1, source_target_pairs={{0,2},{1,3},{2,0},{3,1},{4,6},{5,7},{6,4},{7,5},{8,10},{9,11},{10,... | collective-permute-start | bytes 3145736 | tf_op jit(solution)/shard_map/ppermute | solution.py:151
  265.2 50.4 %collective-permute-start.44 = (bf16[2,128,1024]{2,1,0:T(8,128)(2,1)S(1)}, bf16[2,128,1024]{2,1,0:T(8,128)(2,1)S(1)}, u32[]{:S(2)}, u32[]{:S(2)}) collective-permute-start(bf16[2,128,1024]{2,1,0:T(8,128)(2,1)S(1)} %slice.200), channel_id=1, source_target_pairs={{0,16},{4,20},{8,24},{12,28},{16,0},{20,4},{24,8},{28,12},{1,17},{... | collective-permute-start | bytes 1572872 | tf_op jit(solution)/shard_map/ppermute | solution.py:151
  291.4 42.9 %collective-permute-start.45 = (bf16[2,128,1024]{2,1,0:T(8,128)(2,1)}, bf16[2,128,1024]{2,1,0:T(8,128)(2,1)}, u32[]{:S(2)}, u32[]{:S(2)}) collective-permute-start(bf16[2,128,1024]{2,1,0:T(8,128)(2,1)} %slice.199), channel_id=1, source_target_pairs={{0,16},{4,20},{8,24},{12,28},{16,0},{20,4},{24,8},{28,12},{1,17},{... | collective-permute-start | bytes 1572872 | tf_op jit(solution)/shard_map/ppermute | solution.py:151
  294.2 53.7 %collective-permute-start.47 = (bf16[4,128,1024]{2,1,0:T(8,128)(2,1)}, bf16[4,128,1024]{2,1,0:T(8,128)(2,1)}, u32[]{:S(2)}, u32[]{:S(2)}) collective-permute-start(bf16[4,128,1024]{2,1,0:T(8,128)(2,1)} %weight_grad.24), channel_id=1, source_target_pairs={{0,4},{4,0},{8,12},{12,8},{16,20},{20,16},{24,28},{28,24},{1,5},{5... | collective-permute-start | bytes 3145736 | tf_op jit(solution)/shard_map/ppermute | solution.py:151
  295.8 52.1 %collective-permute-start.48 = (bf16[4,128,1024]{2,1,0:T(8,128)(2,1)}, bf16[4,128,1024]{2,1,0:T(8,128)(2,1)}, u32[]{:S(2)}, u32[]{:S(2)}) collective-permute-start(bf16[4,128,1024]{2,1,0:T(8,128)(2,1)} %add_convert_fusion.1), channel_id=1, source_target_pairs={{0,2},{1,3},{2,0},{3,1},{4,6},{5,7},{6,4},{7,5},{8,10},{9,11},{10,... | collective-permute-start | bytes 3145736 | tf_op jit(solution)/shard_map/ppermute | solution.py:151
  352.7 29.3 %collective-permute-start.54 = (bf16[128,1024]{1,0:T(8,128)(2,1)}, bf16[128,1024]{1,0:T(8,128)(2,1)}, u32[]{:S(2)}, u32[]{:S(2)}) collective-permute-start(bf16[128,1024]{1,0:T(8,128)(2,1)} %get-tuple-element.371), channel_id=1, source_target_pairs={{0,8},{4,12},{8,0},{12,4},{16,24},{20,28},{24,16},{28,20},{1,9},{5... | collective-permute-start | bytes 786440 | tf_op jit(solution)/shard_map/ppermute | solution.py:151
  352.7 29.3 %collective-permute-start.55 = (bf16[128,1024]{1,0:T(8,128)(2,1)}, bf16[128,1024]{1,0:T(8,128)(2,1)}, u32[]{:S(2)}, u32[]{:S(2)}) collective-permute-start(bf16[128,1024]{1,0:T(8,128)(2,1)} %get-tuple-element.370), channel_id=1, source_target_pairs={{0,16},{4,20},{8,24},{12,28},{16,0},{20,4},{24,8},{28,12},{1,17},{... | collective-permute-start | bytes 786440 | tf_op jit(solution)/shard_map/ppermute | solution.py:151
  353.3 28.7 %collective-permute-start.56 = (bf16[128,1024]{1,0:T(8,128)(2,1)}, bf16[128,1024]{1,0:T(8,128)(2,1)}, u32[]{:S(2)}, u32[]{:S(2)}) collective-permute-start(bf16[128,1024]{1,0:T(8,128)(2,1)} %get-tuple-element.369), channel_id=1, source_target_pairs={{0,24},{4,28},{8,16},{12,20},{16,8},{20,12},{24,0},{28,4},{1,25},{... | collective-permute-start | bytes 786440 | tf_op jit(solution)/shard_map/ppermute | solution.py:151
  367.3 29.5 %collective-permute-start.49 = (bf16[256,1024]{1,0:T(8,128)(2,1)S(1)}, bf16[256,1024]{1,0:T(8,128)(2,1)S(1)}, u32[]{:S(2)}, u32[]{:S(2)}) collective-permute-start(bf16[256,1024]{1,0:T(8,128)(2,1)S(1)} %get-tuple-element.368), channel_id=1, source_target_pairs={{0,2},{1,3},{2,0},{3,1},{4,6},{5,7},{6,4},{7,5},{8,10},{9,11},{10,... | collective-permute-start | bytes 1572872 | tf_op jit(solution)/shard_map/ppermute | solution.py:151
  (136 other events, 1133.6 us)
where the time goes:
time: 402 us; the launch traced here: 399 us
  Pallas kernels  157 us (39%)
  waiting for transfers between devices  98.2 us (24%)
  starting transfers between devices  60.3 us (15%)
  local copies, waits for them, and re-layouts  40.8 us (10%)
  other arithmetic  38.1 us (9%)
    pallas_call x30, Pallas kernels, grid_call(): pl.pallas_call(kernel, name=name, grid_spec=pltpu.PrefetchScalarGridSpec(...  108 us
    ppermute x60, waiting for transfers between devices, exchange(): lax.ppermute(value, axis, [(i, i ^ bit) for i in range(lax.axis_size(axis...  98.2 us
    ppermute x60, starting transfers between devices, exchange(): lax.ppermute(value, axis, [(i, i ^ bit) for i in range(lax.axis_size(axis...  60.3 us
    pallas_call x2, Pallas kernels, team_back(): pl.pallas_call(partial(team_back_kernel, part), name='team_back', grid_sp...  25.3 us
    unnamed x216, local copies, waits for them, and re-layouts  18.6 us
    pallas_call x2, Pallas kernels, team_attend(): pl.pallas_call(partial(team_attend_kernel, part), name='team_attend', gri...  16.4 us
  transfers between devices with their start and end apart: 60, of which 30 were waited for; matrix products, arithmetic and copies ran while one was open for 14% of the time, Pallas kernels for 39%

commit v1 on v0

--- a/solution.py
+++ b/solution.py
@@ -472,7 +472,7 @@
     )
 
 
-WORK = pl.CostEstimate(flops=10000000000, bytes_accessed=20000000, transcendentals=0)
+WORK = pl.CostEstimate(flops=4000000000, bytes_accessed=8000000, transcendentals=0)
 
 
 def whole_block(array):

time: 402 us -> 396 us (0.985)
    unnamed x216 -> x200, local copies, waits for them, and re-layouts: 18.6 us -> 16.5 us
  transfers between devices with their start and end apart: 60 -> 60, of which waited for: 30 -> 31; matrix products, arithmetic and copies ran while one was open for 14% -> 13% of each run, Pallas kernels for 39% -> 41%
where the time goes in v1:
time: 396 us; the launch traced here: 392 us
  Pallas kernels  161 us (41%)
  waiting for transfers between devices  94.4 us (24%)
  starting transfers between devices  61.1 us (15%)
  local copies, waits for them, and re-layouts  37.3 us (9%)
  other arithmetic  34.1 us (9%)
    pallas_call x30, Pallas kernels, grid_call(): pl.pallas_call(kernel, name=name, grid_spec=pltpu.PrefetchScalarGridSpec(...  109 us
    ppermute x60, waiting for transfers between devices, exchange(): lax.ppermute(value, axis, [(i, i ^ bit) for i in range(lax.axis_size(axis...  94.4 us
    ppermute x60, starting transfers between devices, exchange(): lax.ppermute(value, axis, [(i, i ^ bit) for i in range(lax.axis_size(axis...  61.1 us
    pallas_call x2, Pallas kernels, team_back(): pl.pallas_call(partial(team_back_kernel, part), name='team_back', grid_sp...  25.2 us
    unnamed x200, local copies, waits for them, and re-layouts  16.5 us
    pallas_call x2, Pallas kernels, team_attend(): pl.pallas_call(partial(team_attend_kernel, part), name='team_attend', gri...  16.5 us
    pallas_call x10, Pallas kernels, joined(): pl.pallas_call(kernel, name='joined', out_shape=shape_of((2 * count, rows...  10.2 us
  transfers between devices with their start and end apart: 60, of which 31 were waited for; matrix products, arithmetic and copies ran while one was open for 13% of the time, Pallas kernels for 41%

profile of v1, /device:TPU:0, one launch (start us, length us, event | category | flops | bytes accessed | tf_op | source)
XLA Modules:
  0.0 391.9 jit_solution(3223432772220707757)
XLA Ops:
  12.0 4.0 %collective-permute-done.15.second_ref = bf16[1,144,768]{2,1,0:T(8,128)(2,1)S(1)} collective-permute-done((bf16[1,144,768]{2,1,0:T(8,128)(2,1)}, bf16[1,144,768]{2,1,0:T(8,128)(2,1)S(1)}, u32[]{:S(2)}, u32[]{:S(2)}) %collective-permute-start.15) | collective-permute-done | bytes 221216 | tf_op jit(solution)/shard_map/ppermute | solution.py:151
  30.4 7.9 %collective-permute-done.17.second_ref = bf16[2,144,768]{2,1,0:T(8,128)(2,1)S(1)} collective-permute-done((bf16[2,144,768]{2,1,0:T(8,128)(2,1)S(1)}, bf16[2,144,768]{2,1,0:T(8,128)(2,1)S(1)}, u32[]{:S(2)}, u32[]{:S(2)}) %collective-permute-start.17) | collective-permute-done | bytes 442400 | tf_op jit(solution)/shard_map/ppermute | solution.py:151
  42.4 4.0 %collective-permute-start.20 = (bf16[1,128,1024]{2,1,0:T(8,128)(2,1)}, bf16[1,128,1024]{2,1,0:T(8,128)(2,1)}, u32[]{:S(2)}, u32[]{:S(2)}) collective-permute-start(bf16[1,128,1024]{2,1,0:T(8,128)(2,1)} %get-tuple-element.263.first_ref), channel_id=1, source_target_pairs={{0,8},{4,12},{8,0},{12,4},{16,24},{20,28},{24,16},{28,20},{1,9},{5... | collective-permute-start | bytes 786440 | tf_op jit(solution)/shard_map/ppermute | solution.py:151
  51.8 3.1 pad_maximum_fusion.rest_0_.lhs_ref
  63.5 3.6 first_norm.1.lhs_ref.left_ref
  71.6 8.2 %team_attend.2 = (bf16[1024,256]{1,0:T(8,128)(2,1)S(1)}, f32[2,8,1024]{2,1,0:T(8,128)S(1)}) custom-call(s32[3]{0:T(128)S(1)} %pad_add_fusion.order, bf16[1024,768]{1,0:T(8,128)(2,1)S(1)} %project.2.q_ref.k_ref.v_ref, bf16[1024,768]{1,0:T(8,128)(2,1)S(1)} %project.2.q_ref.k_ref.v_ref, bf16[1024,768]{1,0:T(8,128)(2,1)S(1)} %project.2.q_ref.k_ref.v_ref), custom_call_target="tpu_custom_call" | custom-call | flops 4000000000 | bytes 8000000 | tf_op jit(solution)/shard_map/team_attend/pallas_call | solution.py:1035
  83.9 3.6 collective-permute-start.28
  89.5 4.0 %project.3.q_ref.k_ref.v_ref = bf16[1024,768]{1,0:T(8,128)(2,1)S(1)} custom-call(s32[3]{0:T(128)S(1)} %pad_add_fusion.order, bf16[1024,1024]{1,0:T(8,128)(2,1)S(1)} %first_norm.1.lhs_ref.left_ref, f32[2,768]{1,0:T(2,128)S(1)} %get-tuple-element.271.bias_ref, bf16[4,144,768]{2,1,0:T(8,128)(2,1)} %collective-permute-done.23.first_ref.rest_8_, ...), custom_call_target="tpu_custom_call" | custom-call | flops 4000000000 | bytes 8000000 | tf_op jit(solution)/shard_map/project/pallas_call | solution.py:564
  93.6 8.2 %team_attend.3 = (bf16[1024,256]{1,0:T(8,128)(2,1)S(1)}, f32[2,8,1024]{2,1,0:T(8,128)S(1)}) custom-call(s32[3]{0:T(128)S(1)} %pad_add_fusion.order, bf16[1024,768]{1,0:T(8,128)(2,1)S(1)} %project.3.q_ref.k_ref.v_ref, bf16[1024,768]{1,0:T(8,128)(2,1)S(1)} %project.3.q_ref.k_ref.v_ref, bf16[1024,768]{1,0:T(8,128)(2,1)S(1)} %project.3.q_ref.k_ref.v_ref), custom_call_target="tpu_custom_call" | custom-call | flops 4000000000 | bytes 8000000 | tf_op jit(solution)/shard_map/team_attend/pallas_call | solution.py:1035
  101.8 7.0 %collective-permute-done.27.second_ref = bf16[2,128,1024]{2,1,0:T(8,128)(2,1)S(1)} collective-permute-done((bf16[2,128,1024]{2,1,0:T(8,128)(2,1)S(1)}, bf16[2,128,1024]{2,1,0:T(8,128)(2,1)S(1)}, u32[]{:S(2)}, u32[]{:S(2)}) %collective-permute-start.27) | collective-permute-done | bytes 524320 | tf_op jit(solution)/shard_map/ppermute | solution.py:151
  122.0 4.0 %out_and_norm.1 = (f32[512,1024]{1,0:T(8,128)S(1)}, bf16[512,1024]{1,0:T(8,128)(2,1)S(1)}) custom-call(s32[3]{0:T(128)S(1)} %pad_add_fusion.order, bf16[512,1024]{1,0:T(8,128)(2,1)S(1)} %pad_maximum_fusion.2.lhs_ref.left_ref, bf16[512,1024]{1,0:T(8,128)(2,1)S(1)} %pad_maximum_fusion.3.tok_ref, f32[16,1024]{1,0:T(8,128)S(1)} %get-tuple-element.267.vec_ref, ...), custom_call_target="tpu_custom_call" | custom-call | flops 4000000000 | bytes 8000000 | tf_op jit(solution)/shard_map/out_and_norm/pallas_call | solution.py:564
  131.6 7.4 %feed_up.2 = (bf16[1024,1024]{1,0:T(8,128)(2,1)S(1)}, bf16[1024,1024]{1,0:T(8,128)(2,1)S(1)}) custom-call(s32[3]{0:T(128)S(1)} %pad_add_fusion.order, bf16[1024,1024]{1,0:T(8,128)(2,1)S(1)} %pad_maximum_fusion.1.lhs_ref.left_ref, f32[2,1024]{1,0:T(2,128)S(1)} %get-tuple-element.296.bias_ref, bf16[4,128,1024]{2,1,0:T(8,128)(2,1)} %joined.15.first_ref.rest_0_, ...), custom_call_target="tpu_custom_call" | custom-call | flops 4000000000 | bytes 8000000 | tf_op jit(solution)/shard_map/feed_up/pallas_call | solution.py:564
  142.4 3.2 weight_grad.13
  145.6 5.8 %feed_down_back.2 = (bf16[1024,1024]{1,0:T(8,128)(2,1)S(1)}, f32[8,1024]{1,0:T(8,128)S(1)}) custom-call(s32[3]{0:T(128)S(1)} %pad_add_fusion.order, bf16[1024,1024]{1,0:T(8,128)(2,1)S(1)} %copy-done.3, bf16[1024,1024]{1,0:T(8,128)(2,1)S(1)} %get-tuple-element.302.slope_ref, bf16[4,128,1024]{2,1,0:T(8,128)(2,1)} %joined.17.first_ref.rest_0_, ...), custom_call_target="tpu_custom_call" | custom-call | flops 4000000000 | bytes 8000000 | tf_op jit(solution)/shard_map/feed_down_back/pallas_call | solution.py:564
  156.6 10.6 %collective-permute-done.33.second_ref.rest_3_ = bf16[4,128,1024]{2,1,0:T(8,128)(2,1)S(1)} collective-permute-done((bf16[4,128,1024]{2,1,0:T(8,128)(2,1)S(1)}, bf16[4,128,1024]{2,1,0:T(8,128)(2,1)S(1)}, u32[]{:S(2)}, u32[]{:S(2)}) %collective-permute-start.33) | collective-permute-done | bytes 1048608 | tf_op jit(solution)/shard_map/ppermute | solution.py:151
  167.1 6.2 %feed_up.3 = (bf16[1024,1024]{1,0:T(8,128)(2,1)S(1)}, bf16[1024,1024]{1,0:T(8,128)(2,1)S(1)}) custom-call(s32[3]{0:T(128)S(1)} %pad_add_fusion.order, bf16[1024,1024]{1,0:T(8,128)(2,1)S(1)} %pad_maximum_fusion.1.lhs_ref.left_ref, f32[2,1024]{1,0:T(2,128)S(1)} %get-tuple-element.296.bias_ref, bf16[4,128,1024]{2,1,0:T(8,128)(2,1)S(1)} %joined.19.first_ref.rest_2_, ...), custom_call_target="tpu_custom_call" | custom-call | flops 4000000000 | bytes 8000000 | tf_op jit(solution)/shard_map/feed_up/pallas_call | solution.py:564
  182.1 5.3 %feed_down_back.3 = (bf16[1024,1024]{1,0:T(8,128)(2,1)S(1)}, f32[8,1024]{1,0:T(8,128)S(1)}) custom-call(s32[3]{0:T(128)S(1)} %pad_add_fusion.order, bf16[1024,1024]{1,0:T(8,128)(2,1)S(1)} %copy-done.3, bf16[1024,1024]{1,0:T(8,128)(2,1)S(1)} %get-tuple-element.311.slope_ref, bf16[4,128,1024]{2,1,0:T(8,128)(2,1)} %collective-permute-done.34.first_ref.rest_2_, ...), custom_call_target="tpu_custom_call" | custom-call | flops 4000000000 | bytes 8000000 | tf_op jit(solution)/shard_map/feed_down_back/pallas_call | solution.py:564
  192.9 8.5 %feed_up_back.1 = (f32[512,1024]{1,0:T(8,128)S(1)}, bf16[512,1024]{1,0:T(8,128)(2,1)}) custom-call(s32[3]{0:T(128)S(1)} %pad_add_fusion.order, bf16[1024,1024]{1,0:T(8,128)(2,1)S(1)} %get-tuple-element.303.rest_0_.first_grad, bf16[1024,1024]{1,0:T(8,128)(2,1)S(1)} %get-tuple-element.312.rest_0_.second_grad, bf16[4,128,1024]{2,1,0:T(8,128)(2,1)} %joined.15.first_ref.rest_0_, ...), custom_call_target="tpu_custom_call" | custom-call | flops 4000000000 | bytes 8000000 | tf_op jit(solution)/shard_map/feed_up_back/pallas_call | solution.py:564
  202.7 3.9 conditional.22
  213.3 6.3 %middle_back.1 = (f32[512,1024]{1,0:T(8,128)S(1)}, bf16[512,1024]{1,0:T(8,128)(2,1)S(1)}, bf16[512,512]{1,0:T(8,128)(2,1)S(1)}, bf16[512,512]{1,0:T(8,128)(2,1)}, f32[4,8,1024]{2,1,0:T(8,128)S(1)}) custom-call(s32[3]{0:T(128)S(1)} %pad_add_fusion.order, f32[512,1024]{1,0:T(8,128)S(1)} %copy-done.38, bf16[512,1024]{1,0:T(8,128)(2,1)S(1)} %copy-done.97, ...), custom_call_target="tpu_custom_call" | custom-call | flops 4000000000 | bytes 8000000 | tf_op jit(solution)/shard_map/middle_back/pallas_call | solution.py:564
  236.0 12.5 %team_back.2 = (bf16[1024,256]{1,0:T(8,128)(2,1)S(1)}, bf16[1024,256]{1,0:T(8,128)(2,1)S(1)}, bf16[1024,256]{1,0:T(8,128)(2,1)S(1)}, f32[2,2,8,128]{3,2,1,0:T(8,128)S(1)}) custom-call(s32[3]{0:T(128)S(1)} %pad_add_fusion.order, bf16[1024,768]{1,0:T(8,128)(2,1)S(1)} %copy-done.55, bf16[1024,768]{1,0:T(8,128)(2,1)S(1)} %copy-done.55, ...), custom_call_target="tpu_custom_call" | custom-call | flops 4000000000 | bytes 8000000 | tf_op jit(solution)/shard_map/team_back/pallas_call | solution.py:1107
  253.9 5.6 %collective-permute-done.40 = bf16[4,128,1024]{2,1,0:T(8,128)(2,1)S(1)} collective-permute-done((bf16[4,128,1024]{2,1,0:T(8,128)(2,1)S(1)}, bf16[4,128,1024]{2,1,0:T(8,128)(2,1)S(1)}, u32[]{:S(2)}, u32[]{:S(2)}) %collective-permute-start.40) | collective-permute-done | bytes 1048608 | tf_op jit(solution)/shard_map/ppermute | solution.py:151
  267.2 12.7 %team_back.3 = (bf16[1024,256]{1,0:T(8,128)(2,1)S(1)}, bf16[1024,256]{1,0:T(8,128)(2,1)S(1)}, bf16[1024,256]{1,0:T(8,128)(2,1)S(1)}, f32[2,2,8,128]{3,2,1,0:T(8,128)S(1)}) custom-call(s32[3]{0:T(128)S(1)} %pad_add_fusion.order, bf16[1024,768]{1,0:T(8,128)(2,1)S(1)} %copy-done.53, bf16[1024,768]{1,0:T(8,128)(2,1)S(1)} %copy-done.53, ...), custom_call_target="tpu_custom_call" | custom-call | flops 4000000000 | bytes 8000000 | tf_op jit(solution)/shard_map/team_back/pallas_call | solution.py:1107
  282.6 3.6 weight_grad.24
  292.1 7.3 %project_back.1 = (f32[512,1024]{1,0:T(8,128)S(1)}, bf16[512,1024]{1,0:T(8,128)(2,1)}) custom-call(s32[3]{0:T(128)S(1)} %pad_add_fusion.order, bf16[1024,256]{1,0:T(8,128)(2,1)S(1)} %get-tuple-element.338.rest_0_, bf16[1024,256]{1,0:T(8,128)(2,1)S(1)} %get-tuple-element.341.rest_1_, bf16[1024,256]{1,0:T(8,128)(2,1)S(1)} %get-tuple-element.342.rest_2_, ...), custom_call_target="tpu_custom_call" | custom-call | flops 4000000000 | bytes 8000000 | tf_op jit(solution)/shard_map/project_back/pallas_call | solution.py:564
  300.7 9.3 %feed_down.1 = (f32[512,1024]{1,0:T(8,128)S(1)}, bf16[512,1024]{1,0:T(8,128)(2,1)}) custom-call(s32[3]{0:T(128)S(1)} %pad_add_fusion.order, bf16[1024,1024]{1,0:T(8,128)(2,1)S(1)} %copy-done.40, bf16[1024,1024]{1,0:T(8,128)(2,1)S(1)} %copy-done.42, bf16[4,128,1024]{2,1,0:T(8,128)(2,1)} %joined.17.first_ref.rest_0_, bf16[4,128,1024]{2,1,0:T(8,128)(2,1)S(1)} %copy-done.24, ...), custom_call_target="tpu_custom_call" | custom-call | flops 4000000000 | bytes 8000000 | tf_op jit(solution)/shard_map/feed_down/pallas_call | solution.py:564
  312.3 3.8 conditional.25
  318.4 4.1 %conditional.26 = (bf16[512,1024]{1,0:T(8,128)(2,1)}) conditional(s32[]{:T(128)} %convert_element_type.138, bf16[512,1024]{1,0:T(8,128)(2,1)} %get-tuple-element.356, bf16[512,1024]{1,0:T(8,128)(2,1)} %get-tuple-element.356), branch_computations={%region_22.23_spmd, %region_23.24_spmd} | conditional | bytes 6291504 | solution.py:1306
  332.2 4.5 %collective-permute-done.43 = bf16[256,1024]{1,0:T(8,128)(2,1)S(1)} collective-permute-done((bf16[256,1024]{1,0:T(8,128)(2,1)S(1)}, bf16[256,1024]{1,0:T(8,128)(2,1)S(1)}, u32[]{:S(2)}, u32[]{:S(2)}) %collective-permute-start.43) | collective-permute-done | bytes 524320 | tf_op jit(solution)/shard_map/ppermute | solution.py:151
  340.6 3.8 fusion.11
  372.3 3.1 collective-permute-done.53
  379.2 4.2 %collective-permute-done.57 = f32[64,1024]{1,0:T(8,128)S(1)} collective-permute-done((f32[64,1024]{1,0:T(8,128)S(1)}, f32[64,1024]{1,0:T(8,128)S(1)}, u32[]{:S(2)}, u32[]{:S(2)}) %collective-permute-start.57) | collective-permute-done | bytes 262176 | tf_op jit(solution)/shard_map/ppermute | solution.py:151
  (432 shorter events, 237.5 us)
Async XLA Ops:
  3.2 22.5 %collective-permute-start.16 = (bf16[256,1024]{1,0:T(8,128)(2,1)}, bf16[256,1024]{1,0:T(8,128)(2,1)}, u32[]{:S(2)}, u32[]{:S(2)}) collective-permute-start(bf16[256,1024]{1,0:T(8,128)(2,1)} %get-tuple-element.374), channel_id=1, source_target_pairs={{0,2},{1,3},{2,0},{3,1},{4,6},{5,7},{6,4},{7,5},{8,10},{9,11},{10,... | collective-permute-start | bytes 1572872 | tf_op jit(solution)/shard_map/ppermute | solution.py:151
  17.0 21.3 %collective-permute-start.17 = (bf16[2,144,768]{2,1,0:T(8,128)(2,1)S(1)}, bf16[2,144,768]{2,1,0:T(8,128)(2,1)S(1)}, u32[]{:S(2)}, u32[]{:S(2)}) collective-permute-start(bf16[2,144,768]{2,1,0:T(8,128)(2,1)S(1)} %joined.10.first_ref), channel_id=1, source_target_pairs={{0,16},{4,20},{8,24},{12,28},{16,0},{20,4},{24,8},{28,12},{1,17},{... | collective-permute-start | bytes 1327112 | tf_op jit(solution)/shard_map/ppermute | solution.py:151
  26.5 20.0 %collective-permute-start.19 = (bf16[256,1024]{1,0:T(8,128)(2,1)}, bf16[256,1024]{1,0:T(8,128)(2,1)}, u32[]{:S(2)}, u32[]{:S(2)}) collective-permute-start(bf16[256,1024]{1,0:T(8,128)(2,1)} %dynamic-slice_bitcast_fusion.2), channel_id=1, source_target_pairs={{0,2},{1,3},{2,0},{3,1},{4,6},{5,7},{6,4},{7,5},{8,10},{9,11},{10,... | collective-permute-start | bytes 1572872 | tf_op jit(solution)/shard_map/ppermute | solution.py:151
  40.4 22.5 %collective-permute-start.22 = (bf16[4,144,768]{2,1,0:T(8,128)(2,1)S(1)}, bf16[4,144,768]{2,1,0:T(8,128)(2,1)S(1)}, u32[]{:S(2)}, u32[]{:S(2)}) collective-permute-start(bf16[4,144,768]{2,1,0:T(8,128)(2,1)S(1)} %joined.11.mine_ref.first_ref.rest_6_), channel_id=1, source_target_pairs={{0,4},{4,0},{8,12},{12,8},{16,20},{20,16},{24,28},{28,24},{1,5},{5... | collective-permute-start | bytes 2654216 | tf_op jit(solution)/shard_map/ppermute | solution.py:151
  41.9 25.2 %collective-permute-start.23 = (bf16[4,144,768]{2,1,0:T(8,128)(2,1)S(1)}, bf16[4,144,768]{2,1,0:T(8,128)(2,1)}, u32[]{:S(2)}, u32[]{:S(2)}) collective-permute-start(bf16[4,144,768]{2,1,0:T(8,128)(2,1)S(1)} %joined.11.mine_ref.first_ref.rest_6_), channel_id=1, source_target_pairs={{0,2},{1,3},{2,0},{3,1},{4,6},{5,7},{6,4},{7,5},{8,10},{9,11},{10,... | collective-permute-start | bytes 2654216 | tf_op jit(solution)/shard_map/ppermute | solution.py:151
  57.1 25.1 %collective-permute-start.24 = (bf16[2,128,1024]{2,1,0:T(8,128)(2,1)S(1)}, bf16[2,128,1024]{2,1,0:T(8,128)(2,1)S(1)}, u32[]{:S(2)}, u32[]{:S(2)}) collective-permute-start(bf16[2,128,1024]{2,1,0:T(8,128)(2,1)S(1)} %joined.13.first_ref), channel_id=1, source_target_pairs={{0,16},{4,20},{8,24},{12,28},{16,0},{20,4},{24,8},{28,12},{1,17},{... | collective-permute-start | bytes 1572872 | tf_op jit(solution)/shard_map/ppermute | solution.py:151
  59.8 53.0 %collective-permute-start.29 = (bf16[4,128,512]{2,1,0:T(8,128)(2,1)S(1)}, bf16[4,128,512]{2,1,0:T(8,128)(2,1)S(1)}, u32[]{:S(2)}, u32[]{:S(2)}) collective-permute-start(bf16[4,128,512]{2,1,0:T(8,128)(2,1)S(1)} %joined.14.rest_0_), channel_id=1, source_target_pairs={{0,4},{4,0},{8,12},{12,8},{16,20},{20,16},{24,28},{28,24},{1,5},{5... | collective-permute-start | bytes 1572872 | tf_op jit(solution)/shard_map/ppermute | solution.py:151
  60.7 22.5 %collective-permute-start.25 = (bf16[1,128,1024]{2,1,0:T(8,128)(2,1)S(1)}, bf16[1,128,1024]{2,1,0:T(8,128)(2,1)S(1)}, u32[]{:S(2)}, u32[]{:S(2)}) collective-permute-start(bf16[1,128,1024]{2,1,0:T(8,128)(2,1)S(1)} %get-tuple-element.279.first_ref), channel_id=1, source_target_pairs={{0,8},{4,12},{8,0},{12,4},{16,24},{20,28},{24,16},{28,20},{1,9},{5... | collective-permute-start | bytes 786440 | tf_op jit(solution)/shard_map/ppermute | solution.py:151
  70.1 19.4 %collective-permute-start.26 = (bf16[4,144,768]{2,1,0:T(8,128)(2,1)S(1)}, bf16[4,144,768]{2,1,0:T(8,128)(2,1)S(1)}, u32[]{:S(2)}, u32[]{:S(2)}) collective-permute-start(bf16[4,144,768]{2,1,0:T(8,128)(2,1)S(1)} %collective-permute-done.22.came_ref.second_ref.rest_7_), channel_id=1, source_target_pairs={{0,2},{1,3},{2,0},{3,1},{4,6},{5,7},{6,4},{7,5},{8,10},{9,11},{10,... | collective-permute-start | bytes 2654216 | tf_op jit(solution)/shard_map/ppermute | solution.py:151
  83.2 25.6 %collective-permute-start.27 = (bf16[2,128,1024]{2,1,0:T(8,128)(2,1)S(1)}, bf16[2,128,1024]{2,1,0:T(8,128)(2,1)S(1)}, u32[]{:S(2)}, u32[]{:S(2)}) collective-permute-start(bf16[2,128,1024]{2,1,0:T(8,128)(2,1)S(1)} %joined.16.first_ref), channel_id=1, source_target_pairs={{0,16},{4,20},{8,24},{12,28},{16,0},{20,4},{24,8},{28,12},{1,17},{... | collective-permute-start | bytes 1572872 | tf_op jit(solution)/shard_map/ppermute | solution.py:151
  83.3 48.3 %collective-permute-start.30 = (bf16[4,128,1024]{2,1,0:T(8,128)(2,1)}, bf16[4,128,1024]{2,1,0:T(8,128)(2,1)}, u32[]{:S(2)}, u32[]{:S(2)}) collective-permute-start(bf16[4,128,1024]{2,1,0:T(8,128)(2,1)} %joined.15.first_ref.rest_0_), channel_id=1, source_target_pairs={{0,4},{4,0},{8,12},{12,8},{16,20},{20,16},{24,28},{28,24},{1,5},{5... | collective-permute-start | bytes 3145736 | tf_op jit(solution)/shard_map/ppermute | solution.py:151
  83.9 26.0 %collective-permute-start.28 = (bf16[1,128,1024]{2,1,0:T(8,128)(2,1)S(1)}, bf16[1,128,1024]{2,1,0:T(8,128)(2,1)S(1)}, u32[]{:S(2)}, u32[]{:S(2)}) collective-permute-start(bf16[1,128,1024]{2,1,0:T(8,128)(2,1)S(1)} %get-tuple-element.288.first_ref), channel_id=1, source_target_pairs={{0,8},{4,12},{8,0},{12,4},{16,24},{20,28},{24,16},{28,20},{1,9},{5... | collective-permute-start | bytes 786440 | tf_op jit(solution)/shard_map/ppermute | solution.py:151
  110.8 28.3 %collective-permute-start.31 = (bf16[2,128,1024]{2,1,0:T(8,128)(2,1)}, bf16[2,128,1024]{2,1,0:T(8,128)(2,1)}, u32[]{:S(2)}, u32[]{:S(2)}) collective-permute-start(bf16[2,128,1024]{2,1,0:T(8,128)(2,1)} %joined.18.first_ref), channel_id=1, source_target_pairs={{0,16},{4,20},{8,24},{12,28},{16,0},{20,4},{24,8},{28,12},{1,17},{... | collective-permute-start | bytes 1572872 | tf_op jit(solution)/shard_map/ppermute | solution.py:151
  110.8 34.9 %collective-permute-start.32 = (bf16[4,128,1024]{2,1,0:T(8,128)(2,1)}, bf16[4,128,1024]{2,1,0:T(8,128)(2,1)S(1)}, u32[]{:S(2)}, u32[]{:S(2)}) collective-permute-start(bf16[4,128,1024]{2,1,0:T(8,128)(2,1)} %joined.17.first_ref.rest_0_), channel_id=1, source_target_pairs={{0,4},{4,0},{8,12},{12,8},{16,20},{20,16},{24,28},{28,24},{1,5},{5... | collective-permute-start | bytes 3145736 | tf_op jit(solution)/shard_map/ppermute | solution.py:151
  111.2 69.9 %collective-permute-start.34 = (bf16[4,128,1024]{2,1,0:T(8,128)(2,1)}, bf16[4,128,1024]{2,1,0:T(8,128)(2,1)}, u32[]{:S(2)}, u32[]{:S(2)}) collective-permute-start(bf16[4,128,1024]{2,1,0:T(8,128)(2,1)} %joined.17.first_ref.rest_0_), channel_id=1, source_target_pairs={{0,2},{1,3},{2,0},{3,1},{4,6},{5,7},{6,4},{7,5},{8,10},{9,11},{10,... | collective-permute-start | bytes 3145736 | tf_op jit(solution)/shard_map/ppermute | solution.py:151
  141.1 26.1 %collective-permute-start.33 = (bf16[4,128,1024]{2,1,0:T(8,128)(2,1)S(1)}, bf16[4,128,1024]{2,1,0:T(8,128)(2,1)S(1)}, u32[]{:S(2)}, u32[]{:S(2)}) collective-permute-start(bf16[4,128,1024]{2,1,0:T(8,128)(2,1)S(1)} %joined.19.first_ref.rest_2_), channel_id=1, source_target_pairs={{0,4},{4,0},{8,12},{12,8},{16,20},{20,16},{24,28},{28,24},{1,5},{5... | collective-permute-start | bytes 3145736 | tf_op jit(solution)/shard_map/ppermute | solution.py:151
  153.3 35.5 %collective-permute-start.36 = (bf16[4,128,1024]{2,1,0:T(8,128)(2,1)S(1)}, bf16[4,128,1024]{2,1,0:T(8,128)(2,1)S(1)}, u32[]{:S(2)}, u32[]{:S(2)}) collective-permute-start(bf16[4,128,1024]{2,1,0:T(8,128)(2,1)S(1)} %weight_grad.14), channel_id=1, source_target_pairs={{0,4},{4,0},{8,12},{12,8},{16,20},{20,16},{24,28},{28,24},{1,5},{5... | collective-permute-start | bytes 3145736 | tf_op jit(solution)/shard_map/ppermute | solution.py:151
  155.9 26.1 %collective-permute-start.35 = (bf16[4,128,1024]{2,1,0:T(8,128)(2,1)S(1)}, bf16[4,128,1024]{2,1,0:T(8,128)(2,1)S(1)}, u32[]{:S(2)}, u32[]{:S(2)}) collective-permute-start(bf16[4,128,1024]{2,1,0:T(8,128)(2,1)S(1)} %copy-done.23), channel_id=1, source_target_pairs={{0,2},{1,3},{2,0},{3,1},{4,6},{5,7},{6,4},{7,5},{8,10},{9,11},{10,... | collective-permute-start | bytes 3145736 | tf_op jit(solution)/shard_map/ppermute | solution.py:151
  176.2 55.3 %collective-permute-start.38 = (bf16[4,128,1024]{2,1,0:T(8,128)(2,1)}, bf16[4,128,1024]{2,1,0:T(8,128)(2,1)}, u32[]{:S(2)}, u32[]{:S(2)}) collective-permute-start(bf16[4,128,1024]{2,1,0:T(8,128)(2,1)} %weight_grad.16), channel_id=1, source_target_pairs={{0,2},{1,3},{2,0},{3,1},{4,6},{5,7},{6,4},{7,5},{8,10},{9,11},{10,... | collective-permute-start | bytes 3145736 | tf_op jit(solution)/shard_map/ppermute | solution.py:151
  179.5 74.4 %collective-permute-start.39 = (bf16[4,128,1024]{2,1,0:T(8,128)(2,1)}, bf16[4,128,1024]{2,1,0:T(8,128)(2,1)}, u32[]{:S(2)}, u32[]{:S(2)}) collective-permute-start(bf16[4,128,1024]{2,1,0:T(8,128)(2,1)} %weight_grad.17), channel_id=1, source_target_pairs={{0,2},{1,3},{2,0},{3,1},{4,6},{5,7},{6,4},{7,5},{8,10},{9,11},{10,... | collective-permute-start | bytes 3145736 | tf_op jit(solution)/shard_map/ppermute | solution.py:151
  191.6 42.7 %collective-permute-start.37 = (bf16[4,128,1024]{2,1,0:T(8,128)(2,1)}, bf16[4,128,1024]{2,1,0:T(8,128)(2,1)}, u32[]{:S(2)}, u32[]{:S(2)}) collective-permute-start(bf16[4,128,1024]{2,1,0:T(8,128)(2,1)} %weight_grad.18), channel_id=1, source_target_pairs={{0,4},{4,0},{8,12},{12,8},{16,20},{20,16},{24,28},{28,24},{1,5},{5... | collective-permute-start | bytes 3145736 | tf_op jit(solution)/shard_map/ppermute | solution.py:151
  233.5 26.1 %collective-permute-start.40 = (bf16[4,128,1024]{2,1,0:T(8,128)(2,1)S(1)}, bf16[4,128,1024]{2,1,0:T(8,128)(2,1)S(1)}, u32[]{:S(2)}, u32[]{:S(2)}) collective-permute-start(bf16[4,128,1024]{2,1,0:T(8,128)(2,1)S(1)} %add_convert_fusion.3), channel_id=1, source_target_pairs={{0,4},{4,0},{8,12},{12,8},{16,20},{20,16},{24,28},{28,24},{1,5},{5... | collective-permute-start | bytes 3145736 | tf_op jit(solution)/shard_map/ppermute | solution.py:151
  251.8 29.5 %collective-permute-start.41 = (bf16[4,128,1024]{2,1,0:T(8,128)(2,1)S(1)}, bf16[4,128,1024]{2,1,0:T(8,128)(2,1)S(1)}, u32[]{:S(2)}, u32[]{:S(2)}) collective-permute-start(bf16[4,128,1024]{2,1,0:T(8,128)(2,1)S(1)} %weight_grad.22), channel_id=1, source_target_pairs={{0,4},{4,0},{8,12},{12,8},{16,20},{20,16},{24,28},{28,24},{1,5},{5... | collective-permute-start | bytes 3145736 | tf_op jit(solution)/shard_map/ppermute | solution.py:151
  253.1 33.2 %collective-permute-start.42 = (bf16[4,128,1024]{2,1,0:T(8,128)(2,1)S(1)}, bf16[4,128,1024]{2,1,0:T(8,128)(2,1)S(1)}, u32[]{:S(2)}, u32[]{:S(2)}) collective-permute-start(bf16[4,128,1024]{2,1,0:T(8,128)(2,1)S(1)} %add_convert_fusion.4), channel_id=1, source_target_pairs={{0,2},{1,3},{2,0},{3,1},{4,6},{5,7},{6,4},{7,5},{8,10},{9,11},{10,... | collective-permute-start | bytes 3145736 | tf_op jit(solution)/shard_map/ppermute | solution.py:151
  261.5 49.9 %collective-permute-start.44 = (bf16[2,128,1024]{2,1,0:T(8,128)(2,1)S(1)}, bf16[2,128,1024]{2,1,0:T(8,128)(2,1)S(1)}, u32[]{:S(2)}, u32[]{:S(2)}) collective-permute-start(bf16[2,128,1024]{2,1,0:T(8,128)(2,1)S(1)} %slice.200), channel_id=1, source_target_pairs={{0,16},{4,20},{8,24},{12,28},{16,0},{20,4},{24,8},{28,12},{1,17},{... | collective-permute-start | bytes 1572872 | tf_op jit(solution)/shard_map/ppermute | solution.py:151
  287.8 38.3 %collective-permute-start.45 = (bf16[2,128,1024]{2,1,0:T(8,128)(2,1)}, bf16[2,128,1024]{2,1,0:T(8,128)(2,1)}, u32[]{:S(2)}, u32[]{:S(2)}) collective-permute-start(bf16[2,128,1024]{2,1,0:T(8,128)(2,1)} %slice.199), channel_id=1, source_target_pairs={{0,16},{4,20},{8,24},{12,28},{16,0},{20,4},{24,8},{28,12},{1,17},{... | collective-permute-start | bytes 1572872 | tf_op jit(solution)/shard_map/ppermute | solution.py:151
  290.8 49.8 %collective-permute-start.47 = (bf16[4,128,1024]{2,1,0:T(8,128)(2,1)}, bf16[4,128,1024]{2,1,0:T(8,128)(2,1)}, u32[]{:S(2)}, u32[]{:S(2)}) collective-permute-start(bf16[4,128,1024]{2,1,0:T(8,128)(2,1)} %weight_grad.24), channel_id=1, source_target_pairs={{0,4},{4,0},{8,12},{12,8},{16,20},{20,16},{24,28},{28,24},{1,5},{5... | collective-permute-start | bytes 3145736 | tf_op jit(solution)/shard_map/ppermute | solution.py:151
  291.6 49.0 %collective-permute-start.48 = (bf16[4,128,1024]{2,1,0:T(8,128)(2,1)}, bf16[4,128,1024]{2,1,0:T(8,128)(2,1)}, u32[]{:S(2)}, u32[]{:S(2)}) collective-permute-start(bf16[4,128,1024]{2,1,0:T(8,128)(2,1)} %add_convert_fusion.1), channel_id=1, source_target_pairs={{0,2},{1,3},{2,0},{3,1},{4,6},{5,7},{6,4},{7,5},{8,10},{9,11},{10,... | collective-permute-start | bytes 3145736 | tf_op jit(solution)/shard_map/ppermute | solution.py:151
  345.3 30.1 %collective-permute-start.54 = (bf16[128,1024]{1,0:T(8,128)(2,1)}, bf16[128,1024]{1,0:T(8,128)(2,1)}, u32[]{:S(2)}, u32[]{:S(2)}) collective-permute-start(bf16[128,1024]{1,0:T(8,128)(2,1)} %get-tuple-element.371), channel_id=1, source_target_pairs={{0,8},{4,12},{8,0},{12,4},{16,24},{20,28},{24,16},{28,20},{1,9},{5... | collective-permute-start | bytes 786440 | tf_op jit(solution)/shard_map/ppermute | solution.py:151
  347.4 28.1 %collective-permute-start.55 = (bf16[128,1024]{1,0:T(8,128)(2,1)}, bf16[128,1024]{1,0:T(8,128)(2,1)}, u32[]{:S(2)}, u32[]{:S(2)}) collective-permute-start(bf16[128,1024]{1,0:T(8,128)(2,1)} %get-tuple-element.370), channel_id=1, source_target_pairs={{0,16},{4,20},{8,24},{12,28},{16,0},{20,4},{24,8},{28,12},{1,17},{... | collective-permute-start | bytes 786440 | tf_op jit(solution)/shard_map/ppermute | solution.py:151
  347.6 27.9 %collective-permute-start.56 = (bf16[128,1024]{1,0:T(8,128)(2,1)}, bf16[128,1024]{1,0:T(8,128)(2,1)}, u32[]{:S(2)}, u32[]{:S(2)}) collective-permute-start(bf16[128,1024]{1,0:T(8,128)(2,1)} %get-tuple-element.369), channel_id=1, source_target_pairs={{0,24},{4,28},{8,16},{12,20},{16,8},{20,12},{24,0},{28,4},{1,25},{... | collective-permute-start | bytes 786440 | tf_op jit(solution)/shard_map/ppermute | solution.py:151
  359.0 31.3 %collective-permute-start.49 = (bf16[256,1024]{1,0:T(8,128)(2,1)S(1)}, bf16[256,1024]{1,0:T(8,128)(2,1)S(1)}, u32[]{:S(2)}, u32[]{:S(2)}) collective-permute-start(bf16[256,1024]{1,0:T(8,128)(2,1)S(1)} %get-tuple-element.368), channel_id=1, source_target_pairs={{0,2},{1,3},{2,0},{3,1},{4,6},{5,7},{6,4},{7,5},{8,10},{9,11},{10,... | collective-permute-start | bytes 1572872 | tf_op jit(solution)/shard_map/ppermute | solution.py:151
  (128 other events, 1028.2 us)
